TPU v7x, 128 devices: a whole 4x4x4 slice. The times are simulated.
128 devices in a mesh: atom: 8 (over x, z_lo), row: 4 (over y), col: 4 (over z_hi, core).
Axes of the slice: x: 4, y: 4, z: 4 (z_hi: 2, z_lo: 2; z = z_hi * 2 + z_lo), core: 2. Of those that a mesh axis runs over, the one named last changes fastest.
Arguments:
- hyper_image: float32 [32, 64, 512], P(None, 'row', 'col'), may hold values from -6 to 6
- warm_codes: float32 [512, 64, 512], P('atom', 'row', 'col'), may hold values from -1.5 to 1.5
- dictionary: float32 [512, 9, 9, 32], P('atom'), may hold values from -6 to 6
- thresholds: float32 [512], P('atom'), may hold values from 0.5 to 5
- velocity: float32 [512, 9, 9, 32], P(('atom', 'row', 'col')), may hold values from -0.012 to 0.012
Outputs:
- new_codes: float32 [512, 64, 512], P('atom', 'row', 'col')
- new_atoms: float32 [512, 9, 9, 32], P(('atom', 'row', 'col'))
- new_velocity: float32 [512, 9, 9, 32], P(('atom', 'row', 'col'))
All inputs are finite; a program needn't handle non-finite values.
Results may differ from a plain program's by a relative error of at most 0.0003.
Values sent between devices are 32-bit elements; how exact they have to be, the bound alone decides.
A program may use at most 64 MiB of HBM per device.

v0:
```python
import math

import jax
import jax.numpy as jnp
from jax import lax
from jax.sharding import PartitionSpec as P

ITERS = 2


PRECISION_HIGH = lax.Precision.HIGHEST
ETA_CODE = 0.05
MOMENTUM = 0.9
LEARN_RATE = 200.0
EPSILON = 1e-06


def padded_2(block, sides, width):
    for axis, dim in sides:
        count = lax.axis_size(axis)
        forward = [(i, i + 1) for i in range(count - 1)]
        backward = [(target, source) for source, target in forward]
        low = lax.ppermute(
            lax.slice_in_dim(block, block.shape[dim] - width, None, axis=dim), axis, forward
        )
        high = lax.ppermute(lax.slice_in_dim(block, 0, width, axis=dim), axis, backward)
        block = jnp.concatenate([low, block, high], axis=dim)
    return block


def forward_image(padded, dictionary):
    atom_side = dictionary.shape[1]
    row_count = padded.shape[1] - atom_side + 1
    col_count = padded.shape[2] - atom_side + 1
    channels = dictionary.shape[3]

    def forward_row_step(offset_row, accumulated):
        strip_rows = lax.dynamic_slice_in_dim(padded, offset_row, row_count, 1)
        tap_row = lax.dynamic_index_in_dim(dictionary, offset_row, 1, keepdims=False)
        for offset_col in range(atom_side):
            accumulated = accumulated + jnp.einsum(
                "kc,khw->chw",
                tap_row[:, offset_col, :],
                strip_rows[:, :, offset_col : offset_col + col_count],
                precision=PRECISION_HIGH,
                preferred_element_type=jnp.float32,
            )
        return accumulated

    initial = jnp.zeros((channels, row_count, col_count), jnp.float32)
    accumulated = lax.fori_loop(0, atom_side, forward_row_step, initial)
    return accumulated * (1.0 / math.sqrt(atom_side * atom_side * channels))


def adjoint_map(padded_err, dictionary):
    atom_side = dictionary.shape[1]
    margin = atom_side - 1
    row_count = padded_err.shape[1] - margin
    col_count = padded_err.shape[2] - margin
    channels = dictionary.shape[3]

    def adjoint_row_step(offset_row, accumulated):
        strip_rows = lax.dynamic_slice_in_dim(padded_err, margin - offset_row, row_count, 1)
        tap_row = lax.dynamic_index_in_dim(dictionary, offset_row, 1, keepdims=False)
        for offset_col in range(atom_side):
            accumulated = accumulated + jnp.einsum(
                "kc,chw->khw",
                tap_row[:, offset_col, :],
                strip_rows[:, :, margin - offset_col : margin - offset_col + col_count],
                precision=PRECISION_HIGH,
                preferred_element_type=jnp.float32,
            )
        return accumulated

    initial = jnp.zeros((dictionary.shape[0], row_count, col_count), jnp.float32)
    accumulated = lax.fori_loop(0, atom_side, adjoint_row_step, initial)
    return accumulated * (1.0 / math.sqrt(atom_side * atom_side * channels))


def correlate(error_field, padded_codes, row_total, atom_side):
    row_count = error_field.shape[1]
    col_count = error_field.shape[2]
    tap_terms = []
    for offset_row in range(atom_side):
        for offset_col in range(atom_side):
            tap_terms.append(
                jnp.einsum(
                    "chw,khw->kc",
                    error_field,
                    padded_codes[
                        :, offset_row : offset_row + row_count, offset_col : offset_col + col_count
                    ],
                    precision=PRECISION_HIGH,
                    preferred_element_type=jnp.float32,
                )
            )
    stacked = jnp.stack(tap_terms, axis=1)
    return stacked.reshape(row_total, atom_side, atom_side, error_field.shape[0])


def shrink_step(code_field, gradient, thresholds):
    shifted_codes = code_field - ETA_CODE * gradient
    threshold_level = ETA_CODE * thresholds[:, None, None]
    return jnp.sign(shifted_codes) * jnp.maximum(jnp.abs(shifted_codes) - threshold_level, 0.0)


def shards(hyper_image, warm_codes, dictionary, thresholds, velocity):
    atom_side = dictionary.shape[1]
    rim_width = atom_side // 2
    local_atoms = dictionary.shape[0]

    def code_rim(code_field):
        return padded_2(code_field, (("row", 1), ("col", 2)), rim_width)

    def residual_whole(padded_codes):
        summed = lax.psum(forward_image(padded_codes, dictionary), "atom")
        return summed - hyper_image

    current = warm_codes
    for iteration in range(ITERS):
        padded_codes = code_rim(current)
        error_field = residual_whole(padded_codes)
        padded_err = padded_2(error_field, (("row", 1), ("col", 2)), rim_width)
        gradient = adjoint_map(padded_err, dictionary)
        current = shrink_step(current, gradient, thresholds)
    padded_codes = code_rim(current)
    error_field = residual_whole(padded_codes)
    owned_count = velocity.shape[0]
    owned_start = lax.axis_index(("row", "col")) * owned_count
    old_atoms = lax.dynamic_slice_in_dim(dictionary, owned_start, owned_count, 0)
    summed = lax.psum(correlate(error_field, padded_codes, local_atoms, atom_side), ("row", "col"))
    owned_sum = lax.dynamic_slice_in_dim(summed, owned_start, owned_count, 0)
    pixels = (
        error_field.shape[1] * error_field.shape[2] * lax.axis_size("row") * lax.axis_size("col")
    )
    new_velocity = MOMENTUM * velocity + owned_sum / pixels
    stepped = old_atoms - LEARN_RATE * new_velocity
    mean_square = jnp.mean(stepped * stepped, axis=(1, 2, 3), keepdims=True)
    new_atoms = stepped * lax.rsqrt(mean_square + EPSILON)
    return (current, new_atoms, new_velocity)


def solution(mesh):
    in_specs = (
        P(None, "row", "col"),
        P("atom", "row", "col"),
        P("atom", None, None, None),
        P("atom"),
        P(("atom", "row", "col"), None, None, None),
    )
    out_specs = (
        P("atom", "row", "col"),
        P(("atom", "row", "col"), None, None, None),
        P(("atom", "row", "col"), None, None, None),
    )
    return jax.shard_map(shards, mesh=mesh, in_specs=in_specs, out_specs=out_specs, check_vma=False)
```

profile of v0, /device:TPU:1, one launch (start us, length us, event | category | flops | bytes accessed | tf_op | source)
XLA Modules:
  0.0 851.0 jit_solution(1575648235294794534)
XLA Ops:
  7.2 1.6 copy.18
  8.9 4.0 collective-permute-start
  14.2 3.7 collective-permute-done
  17.9 3.8 collective-permute-done.1
  21.8 7.2 collective-permute-start.2
  29.0 1.9 collective-permute-start.3
  30.9 5.1 collective-permute-done.3
  37.1 1.5 copy.21
  38.6 53.3 %while.74 = (s32[]{:T(128)}, f32[32,16,128]{2,0,1:T(8,128)S(1)}, f32[64,9,9,32]{0,3,2,1:T(8,128)}, f32[64,24,136]{2,0,1:T(8,128)S(1)}, s32[]{:T(128)}, /*index=5...) while((s32[]{:T(128)}, f32[32,16,128]{2,0,1:T(8,128)S(1)}, ...), condition=%wide.region_1.2_spmd.clone, body=%wide.region_0.1_spmd.clone.sunk | while | flops 453640192 | bytes 9732407 | solution.py:51
  92.7 67.6 %all-reduce.5.cloned.1.call-done = f32[32,16,128]{2,0,1:T(8,128)} async-done(((f32[32,16,128]{2,0,1:T(8,128)}), f32[32,16,128]{2,0,1:T(8,128)}) %all-reduce.5.cloned.1.call-update) | async-done | bytes 262160 | tf_op jit(solution)/shard_map/psum | solution.py:116
  161.4 3.2 collective-permute-start.4
  164.6 1.3 collective-permute-start.5
  165.9 3.7 collective-permute-done.5
  169.8 11.7 %collective-permute-start.6 = (f32[32,24,4]{2,0,1:T(8,128)S(1)}, f32[32,24,4]{2,0,1:T(8,128)S(1)}, u32[]{:S(2)}, u32[]{:S(2)}) collective-permute-start(f32[32,24,4]{2,0,1:T(8,128)S(1)} %get-tuple-element.608), channel_id=1, source_target_pairs={{0,1},{1,2},{2,3},{4,5},{5,6},{6,7},{8,9},{9,10},{10,11},{12,13},{... | collective-permute-start | bytes 36872 | tf_op jit(solution)/shard_map/ppermute | solution.py:23
  181.5 2.4 collective-permute-start.7
  184.0 2.2 collective-permute-done.6
  186.2 5.9 collective-permute-done.7
  192.5 63.2 %while.75 = (s32[]{:T(128)}, f32[64,16,128]{2,0,1:T(8,128)S(1)}, f32[64,9,9,32]{0,3,2,1:T(8,128)}, f32[32,24,136]{2,0,1:T(8,128)S(1)}, s32[]{:T(128)}, /*index=5...) while((s32[]{:T(128)}, f32[64,16,128]{2,0,1:T(8,128)S(1)}, ...), condition=%wide.region_4.5_spmd.clone, body=%wide.region_3.4_spmd.clone.sunk | while | flops 454295552 | bytes 12091765 | solution.py:76
  255.7 1.3 maximum_multiply_fusion.1
  257.1 3.1 collective-permute-start.8
  260.3 1.3 collective-permute-start.9
  262.2 3.8 collective-permute-done.9
  267.3 3.2 collective-permute-start.10
  270.8 2.1 collective-permute-start.11
  273.2 4.5 collective-permute-done.11
  278.9 1.8 pad_maximum_fusion.1
  280.7 53.3 %while.76 = (s32[]{:T(128)}, f32[32,16,128]{2,0,1:T(8,128)S(1)}, f32[64,9,9,32]{0,3,2,1:T(8,128)}, f32[64,24,136]{2,0,1:T(8,128)S(1)}, s32[]{:T(128)}, /*index=5...) while((s32[]{:T(128)}, f32[32,16,128]{2,0,1:T(8,128)S(1)}, ...), condition=%wide.region_6.7_spmd.clone, body=%wide.region_5.6_spmd.clone.sunk | while | flops 453640192 | bytes 9732407 | solution.py:51
  334.8 63.7 %all-reduce.7.cloned.1.call-done = f32[32,16,128]{2,0,1:T(8,128)} async-done(((f32[32,16,128]{2,0,1:T(8,128)}), f32[32,16,128]{2,0,1:T(8,128)}) %all-reduce.7.cloned.1.call-update) | async-done | bytes 262160 | tf_op jit(solution)/shard_map/psum | solution.py:116
  399.6 3.2 collective-permute-start.12
  404.1 3.7 collective-permute-done.13
  408.0 11.7 %collective-permute-start.14 = (f32[32,24,4]{2,0,1:T(8,128)S(1)}, f32[32,24,4]{2,0,1:T(8,128)S(1)}, u32[]{:S(2)}, u32[]{:S(2)}) collective-permute-start(f32[32,24,4]{2,0,1:T(8,128)S(1)} %get-tuple-element.606), channel_id=1, source_target_pairs={{0,1},{1,2},{2,3},{4,5},{5,6},{6,7},{8,9},{9,10},{10,11},{12,13},{... | collective-permute-start | bytes 36872 | tf_op jit(solution)/shard_map/ppermute | solution.py:23
  419.7 1.9 collective-permute-start.15
  421.7 2.8 collective-permute-done.14
  424.4 5.9 collective-permute-done.15
  430.7 63.2 %while.77 = (s32[]{:T(128)}, f32[64,16,128]{2,0,1:T(8,128)S(1)}, f32[64,9,9,32]{0,3,2,1:T(8,128)}, f32[32,24,136]{2,0,1:T(8,128)S(1)}, s32[]{:T(128)}, /*index=5...) while((s32[]{:T(128)}, f32[64,16,128]{2,0,1:T(8,128)S(1)}, ...), condition=%wide.region_9.10_spmd.clone, body=%wide.region_8.9_spmd.clone.sunk | while | flops 454295552 | bytes 12091765 | solution.py:76
  494.2 3.1 collective-permute-start.16
  497.3 1.7 collective-permute-start.17
  499.3 3.8 collective-permute-done.17
  503.7 3.2 collective-permute-start.18
  507.2 1.9 collective-permute-start.19
  509.5 4.6 collective-permute-done.19
  515.4 1.8 pad_maximum_fusion.2
  517.2 53.2 %while.78 = (s32[]{:T(128)}, f32[32,16,128]{2,0,1:T(8,128)S(1)}, f32[64,9,9,32]{0,3,2,1:T(8,128)}, f32[64,24,136]{2,0,1:T(8,128)S(1)}, s32[]{:T(128)}, /*index=5...) while((s32[]{:T(128)}, f32[32,16,128]{2,0,1:T(8,128)S(1)}, ...), condition=%wide.region_11.12_spmd.clone, body=%wide.region_10.11_spmd.clone.sunk | while | flops 453640192 | bytes 9732407 | solution.py:51
  571.2 2.2 pad_maximum_fusion.3
  573.5 61.5 %all-reduce.9.cloned.1.call-done = f32[32,16,128]{2,0,1:T(8,128)} async-done(((f32[32,16,128]{2,0,1:T(8,128)}), f32[32,16,128]{2,0,1:T(8,128)}) %all-reduce.9.cloned.1.call-update) | async-done | bytes 262160 | tf_op jit(solution)/shard_map/psum | solution.py:116
  686.7 3.1 copy.37
  689.8 1.7 constant_dynamic-slice_fusion
  693.7 148.5 %all-reduce.11.cloned.1.call-done = f32[64,9,9,32]{3,0,2,1:T(8,128)} async-done(((f32[64,9,9,32]{3,0,2,1:T(8,128)}), f32[64,9,9,32]{3,0,2,1:T(8,128)}) %all-reduce.11.cloned.1.call-update) | async-done | bytes 663568 | tf_op jit(solution)/shard_map/psum | solution.py:131
  (611 shorter events, 353.4 us)
Async XLA Ops:
  7.2 153.2 %all-reduce.5.cloned.1.call-start = ((), (), s32[]{:S(2)}) async-start(), calls=%async_computation | async-start | bytes 524288 | tf_op jit(solution)/shard_map/psum | solution.py:116
  8.9 9.0 %collective-permute-start = (f32[64,4,128]{0,1,2:T(4,128)S(1)}, f32[64,4,128]{0,1,2:T(4,128)S(1)}, u32[]{:S(2)}, u32[]{:S(2)}) collective-permute-start(f32[64,4,128]{0,1,2:T(4,128)S(1)} %get-tuple-element.594), channel_id=1, source_target_pairs={{0,4},{4,8},{8,12},{1,5},{5,9},{9,13},{2,6},{6,10},{10,14},{3,7},{... | collective-permute-start | bytes 393224 | tf_op jit(solution)/shard_map/ppermute | solution.py:23
  12.9 8.8 %collective-permute-start.1 = (f32[64,4,128]{0,1,2:T(4,128)S(1)}, f32[64,4,128]{0,1,2:T(4,128)S(1)}, u32[]{:S(2)}, u32[]{:S(2)}) collective-permute-start(f32[64,4,128]{0,1,2:T(4,128)S(1)} %get-tuple-element.595), channel_id=1, source_target_pairs={{4,0},{8,4},{12,8},{5,1},{9,5},{13,9},{6,2},{10,6},{14,10},{7,3},{... | collective-permute-start | bytes 393224 | tf_op jit(solution)/shard_map/ppermute | solution.py:26
  21.8 9.1 %collective-permute-start.2 = (f32[64,24,4]{0,1,2:T(8,128)S(1)}, f32[64,24,4]{0,1,2:T(8,128)S(1)}, u32[]{:S(2)}, u32[]{:S(2)}) collective-permute-start(f32[64,24,4]{0,1,2:T(8,128)S(1)} %get-tuple-element.592), channel_id=1, source_target_pairs={{0,1},{1,2},{2,3},{4,5},{5,6},{6,7},{8,9},{9,10},{10,11},{12,13},{... | collective-permute-start | bytes 73736 | tf_op jit(solution)/shard_map/ppermute | solution.py:23
  29.0 7.0 collective-permute-start.3
  38.6 121.7 %copy-start.4 = (f32[32,16,128]{2,1,0:T(8,128)S(1)}, f32[32,16,128]{2,1,0:T(8,128)}, u32[]{:S(2)}) copy-start(f32[32,16,128]{2,1,0:T(8,128)} %param.15) | copy-start | bytes 786436
  92.7 305.9 %all-reduce.7.cloned.1.call-start = ((), (), s32[]{:S(2)}) async-start(), calls=%async_computation.1 | async-start | bytes 524288 | tf_op jit(solution)/shard_map/psum | solution.py:116
  161.4 22.6 %copy-start.9 = (f32[64]{0:T(128)S(1)}, f32[64]{0:T(128)}, u32[]{:S(2)}) copy-start(f32[64]{0:T(128)} %param.18) | copy-start | bytes 772
  161.4 4.5 collective-permute-start.4
  164.6 5.0 collective-permute-start.5
  169.8 16.4 %collective-permute-start.6 = (f32[32,24,4]{2,0,1:T(8,128)S(1)}, f32[32,24,4]{2,0,1:T(8,128)S(1)}, u32[]{:S(2)}, u32[]{:S(2)}) collective-permute-start(f32[32,24,4]{2,0,1:T(8,128)S(1)} %get-tuple-element.608), channel_id=1, source_target_pairs={{0,1},{1,2},{2,3},{4,5},{5,6},{6,7},{8,9},{9,10},{10,11},{12,13},{... | collective-permute-start | bytes 36872 | tf_op jit(solution)/shard_map/ppermute | solution.py:23
  181.5 10.6 %collective-permute-start.7 = (f32[32,24,4]{2,0,1:T(8,128)S(1)}, f32[32,24,4]{2,0,1:T(8,128)S(1)}, u32[]{:S(2)}, u32[]{:S(2)}) collective-permute-start(f32[32,24,4]{2,0,1:T(8,128)S(1)} %get-tuple-element.609), channel_id=1, source_target_pairs={{1,0},{2,1},{3,2},{5,4},{6,5},{7,6},{9,8},{10,9},{11,10},{13,12},{... | collective-permute-start | bytes 36872 | tf_op jit(solution)/shard_map/ppermute | solution.py:26
  257.1 5.0 collective-permute-start.8
  260.3 5.7 collective-permute-start.9
  266.0 0.7 copy-start.7
  267.3 5.6 collective-permute-start.10
  270.8 6.9 collective-permute-start.11
  334.8 300.2 %all-reduce.9.cloned.1.call-start = ((), (), s32[]{:S(2)}) async-start(), calls=%async_computation.2 | async-start | bytes 524288 | tf_op jit(solution)/shard_map/psum | solution.py:116
  399.6 4.5 collective-permute-start.12
  402.8 5.0 collective-permute-start.13
  408.0 16.4 %collective-permute-start.14 = (f32[32,24,4]{2,0,1:T(8,128)S(1)}, f32[32,24,4]{2,0,1:T(8,128)S(1)}, u32[]{:S(2)}, u32[]{:S(2)}) collective-permute-start(f32[32,24,4]{2,0,1:T(8,128)S(1)} %get-tuple-element.606), channel_id=1, source_target_pairs={{0,1},{1,2},{2,3},{4,5},{5,6},{6,7},{8,9},{9,10},{10,11},{12,13},{... | collective-permute-start | bytes 36872 | tf_op jit(solution)/shard_map/ppermute | solution.py:23
  419.7 10.6 %collective-permute-start.15 = (f32[32,24,4]{2,0,1:T(8,128)S(1)}, f32[32,24,4]{2,0,1:T(8,128)S(1)}, u32[]{:S(2)}, u32[]{:S(2)}) collective-permute-start(f32[32,24,4]{2,0,1:T(8,128)S(1)} %get-tuple-element.607), channel_id=1, source_target_pairs={{1,0},{2,1},{3,2},{5,4},{6,5},{7,6},{9,8},{10,9},{11,10},{13,12},{... | collective-permute-start | bytes 36872 | tf_op jit(solution)/shard_map/ppermute | solution.py:26
  494.2 21.2 %copy-start = (f32[64,16,128]{2,0,1:T(8,128)}, f32[64,16,128]{2,0,1:T(8,128)S(1)}, u32[]{:S(2)}) copy-start(f32[64,16,128]{2,0,1:T(8,128)S(1)} %maximum_multiply_fusion) | copy-start | bytes 1572868
  494.2 5.1 collective-permute-start.16
  497.3 5.7 collective-permute-start.17
  503.7 5.4 collective-permute-start.18
  507.2 6.9 collective-permute-start.19
  509.5 7.7 copy-start.3
  571.2 271.0 %all-reduce.11.cloned.1.call-start = ((), (), s32[]{:S(2)}) async-start(), calls=%async_computation.3 | async-start | bytes 5308416 | tf_op jit(solution)/shard_map/psum | solution.py:131
  636.6 1.9 copy-start.1
  685.6 1.1 copy-start.5
  691.6 1.0 copy-start.2
  691.6 150.6 %copy-start.8 = (f32[4,9,9,32]{3,0,2,1:T(4,128)S(1)}, f32[4,9,9,32]{3,0,2,1:T(4,128)}, u32[]{:S(2)}) copy-start(f32[4,9,9,32]{3,0,2,1:T(4,128)} %param.19) | copy-start | bytes 124420
  843.4 0.8 copy-start.6
Sparse Core Ops, SparseCore 0:
  92.8 67.4 all-reduce.4
  334.9 63.6 all-reduce.6
  571.3 63.6 all-reduce.8
  690.0 152.1 all-reduce.10
where the time goes:
time: 858 us; the launch traced here: 851 us
  waiting for transfers between devices  396 us (46%)
  matrix products  289 us (34%)
  starting transfers between devices  70.9 us (8%)
  local copies, waits for them, and re-layouts  58.8 us (7%)
  other arithmetic  16.9 us (2%)
  between operations  15.2 us (2%)
    psum x3, waiting for transfers between devices, residual_whole(): summed = lax.psum(forward_image(padded_codes, dictionary), 'atom')  193 us
    psum x1, waiting for transfers between devices, shards(): lax.psum(correlate(error_field, padded_codes, local_atoms, atom_side), ('...  148 us
    dot_general x243, matrix products, forward_row_step(): jnp.einsum('kc,khw->chw', tap_row[:, offset_col, :], strip_rows[:, :, off...  132 us
    dot_general x162, matrix products, adjoint_row_step(): jnp.einsum('kc,chw->khw', tap_row[:, offset_col, :], strip_rows[:, :, mar...  108 us
    ppermute x10, starting transfers between devices, padded_2(): lax.ppermute(lax.slice_in_dim(block, block.shape[dim] - width, None, axis...  53.6 us
    dot_general x81, matrix products, correlate(): jnp.einsum('chw,khw->kc', error_field, padded_codes[:, offset_row:offset_...  48.9 us
    ppermute x10, waiting for transfers between devices, padded_2(): lax.ppermute(lax.slice_in_dim(block, 0, width, axis=dim), axis, backward)  44.8 us
    squeeze x27, local copies, waits for them, and re-layouts, forward_row_step(): lax.dynamic_index_in_dim(dictionary, offset_row, 1, keepdims=False)  25 us
  transfers between devices with their start and end apart: 24, of which 19 were waited for; matrix products, arithmetic and copies ran while one was open for 1% of the time, Pallas kernels for 0%

commit v1 on v0

v1 whole, which is shorter than its diff:
```python
import functools
import math

import jax
import jax.numpy as jnp
from jax import lax
from jax.experimental import pallas as pl
from jax.experimental.pallas import tpu as pltpu
from jax.sharding import PartitionSpec as P

ITERS = 2
ETA_CODE = 0.05
MOMENTUM = 0.9
LEARN_RATE = 200.0
EPSILON = 1e-06

F32 = jnp.float32
BF16 = jnp.bfloat16
MESH = pl.DeviceIdType.MESH
VMEM = pl.BlockSpec(memory_space=pltpu.VMEM)
ANY = pl.BlockSpec(memory_space=pl.ANY)

C = 32
T = 9
KL = 64
ROWS = 16
LANES = 128
EXT = ROWS + 8
SLOTS = EXT + 2
SCALE = 1.0 / math.sqrt(T * T * C)


def split(x):
    hi = x.astype(BF16)
    return hi, (x - hi.astype(F32)).astype(BF16)


def lane_index(rows):
    return lax.broadcasted_iota(jnp.int32, (rows, LANES), 1)


def roll(x, shift):
    return pltpu.roll(x, shift % LANES, 1) if shift % LANES else x


def inside(lane, shift):
    return lane >= shift if shift > 0 else lane < LANES + shift


def synthesis(codes, ws, zbuf, acc, part):
    owners = part.shape[0]
    share = C // owners
    lane = lane_index(C)
    zero_rows = jnp.zeros((3 * KL, 2 * LANES), BF16)
    zbuf[0 : 3 * KL] = zero_rows
    zbuf[9 * 3 * KL : 10 * 3 * KL] = zero_rows
    for t in range(8):
        hi, lo = split(jnp.concatenate([codes[t], codes[t + 8]], axis=1))
        base = (t + 1) * 3 * KL
        zbuf[base : base + KL] = hi
        zbuf[base + KL : base + 2 * KL] = lo
        zbuf[base + 2 * KL : base + 3 * KL] = hi
    rims = [jnp.zeros((C, LANES), F32), jnp.zeros((C, LANES), F32)]

    def put(slot, row):
        for q in range(owners):
            part[q, slot] = row[q * share : (q + 1) * share]

    for ho in range(16):
        first, last = max(0, 8 - ho) // 2, min(8, 15 - ho) // 2
        depth = (last - first + 1) * 6 * KL
        start = (2 * first + ho - 7) * 3 * KL
        taps = jnp.dot(
            ws[:, first * 6 * KL : first * 6 * KL + depth],
            zbuf[start : start + depth],
            preferred_element_type=F32,
        )
        for half in range(2):
            main = jnp.zeros((C, LANES), F32)
            rim = jnp.zeros((C, LANES), F32)
            for b in range(T):
                moved = roll(taps[b * C : (b + 1) * C, half * LANES : (half + 1) * LANES], 4 - b)
                if b == 4:
                    main = main + moved
                else:
                    keep = inside(lane, 4 - b)
                    main = main + jnp.where(keep, moved, 0.0)
                    rim = rim + jnp.where(keep, 0.0, moved)
            row = ho + 8 * half
            rims[row // 16] = rims[row // 16] + roll(rim, 8 * (row % 16) + 4)
            if half == 0 and ho >= 8:
                main = main + acc[ho - 8]
            if half == 1 and ho < 8:
                acc[ho] = main
            else:
                put(row + 1, main)
    put(0, rims[0])
    put(SLOTS - 1, rims[1])


def gathered(err, slot):
    return jnp.concatenate([err[q, slot] for q in range(err.shape[0])], axis=0)


def adjoint_step(err, wa, level, codes, ebuf, hbuf, qbuf, gbuf, new_codes):
    wide = 3 * C
    lane_c = lane_index(C)
    lane = lane_index(KL)
    spot = lane % 8
    for row in range(EXT):
        hi, lo = split(gathered(err, row + 1))
        for t, side in ((row, 0), (row - 8, 1)):
            if 0 <= t < 16:
                cols = slice(side * LANES, (side + 1) * LANES)
                ebuf[t * wide : t * wide + C, cols] = hi
                ebuf[t * wide + C : t * wide + 2 * C, cols] = lo
                ebuf[t * wide + 2 * C : t * wide + 3 * C, cols] = hi
    rims = [gathered(err, 0), gathered(err, SLOTS - 1)]
    for t in range(T):
        hi, lo = split(
            jnp.where(lane_c < LANES - 8 * t, roll(rims[0], -8 * t), roll(rims[1], -8 * t))
        )
        hbuf[t * wide : t * wide + C] = hi
        hbuf[t * wide + C : t * wide + 2 * C] = lo
        hbuf[t * wide + 2 * C : t * wide + 3 * C] = hi
    qbuf[:, 0:LANES] = jnp.dot(wa[...], hbuf[...], preferred_element_type=F32)
    edge = jnp.zeros((KL, LANES), F32)
    for b in range(T):
        s = b - 4
        if s == 0:
            continue
        keep = (spot >= 4) & (spot < 4 + s) if s > 0 else (spot < 4) & (spot >= 4 + s)
        edge = edge + jnp.where(keep, roll(qbuf[b * KL : (b + 1) * KL, 0:LANES], s), 0.0)
    gbuf[...] = edge
    ends = (lane < 4) | (lane >= LANES - 4)
    bound = level[...]
    for i in range(8):
        qbuf[...] = jnp.dot(
            wa[...], ebuf[i * wide : (i + T) * wide], preferred_element_type=F32
        )
        for half in range(2):
            row = i + 8 * half
            total = jnp.where(ends, roll(gbuf[...], -(8 * row + 4)), 0.0)
            for b in range(T):
                moved = roll(qbuf[b * KL : (b + 1) * KL, half * LANES : (half + 1) * LANES], b - 4)
                if b != 4:
                    moved = jnp.where(inside(lane, b - 4), moved, 0.0)
                total = total + moved
            shifted = codes[row] - (ETA_CODE * SCALE) * total
            new_codes[row] = shifted - jnp.clip(shifted, -bound, bound)


def correlation(err, codes, lbuf, cbuf, gacc, parts):
    lane = lane_index(C)
    rims = [gathered(err, 0), gathered(err, SLOTS - 1)]
    for row in range(EXT):
        main = gathered(err, row + 1)
        rim = roll(rims[row // 16], -(8 * (row % 16) + 4))
        for b in range(T):
            s = b - 4
            if s > 0:
                field = jnp.where(lane >= LANES - s, rim, main)
            elif s < 0:
                field = jnp.where(lane < -s, rim, main)
            else:
                field = main
            hi, lo = split(roll(field, s))
            at = row * 3 * LANES
            lbuf[b * C : (b + 1) * C, at : at + LANES] = hi
            lbuf[b * C : (b + 1) * C, at + LANES : at + 2 * LANES] = hi
            lbuf[b * C : (b + 1) * C, at + 2 * LANES : at + 3 * LANES] = lo
    none = jnp.zeros((KL, 3 * LANES), BF16)
    cbuf[0:KL, 0 : 3 * LANES] = none
    cbuf[ROWS * KL : (ROWS + 1) * KL, 3 * LANES : 6 * LANES] = none
    for i in range(ROWS):
        hi, lo = split(codes[i])
        for at, base in (((i + 1) * KL, 0), (i * KL, 3 * LANES)):
            cbuf[at : at + KL, base : base + LANES] = hi
            cbuf[at : at + KL, base + LANES : base + 2 * LANES] = lo
            cbuf[at : at + KL, base + 2 * LANES : base + 3 * LANES] = hi
    gacc[...] = jnp.zeros_like(gacc)
    for row in range(0, EXT, 2):
        low, high = max(row - 8, -1), min(row, ROWS - 1)
        a = low - row + 8
        count = (high - low + 1) * KL
        gacc[a * KL : a * KL + count] += lax.dot_general(
            cbuf[(low + 1) * KL : (low + 1) * KL + count],
            lbuf[:, row * 3 * LANES : (row + 2) * 3 * LANES],
            (((1,), (1,)), ((), ())),
            preferred_element_type=F32,
        )
    groups, share = parts.shape[1], parts.shape[3]
    for core in range(2):
        for g in range(groups):
            for a in range(T):
                at = a * KL + (2 * g + core) * share
                parts[core, g, a] = gacc[at : at + share]


def first_kernel(warm, ws, codes, part, zbuf, acc, sem):
    copies = [pltpu.make_async_copy(warm.at[:, i], codes.at[i], sem.at[i]) for i in range(ROWS)]
    for copy in copies:
        copy.start()
    for copy in copies:
        copy.wait()
    synthesis(codes, ws, zbuf, acc, part)


def step_kernel(err, wa, ws, level, codes, new_codes, part, ebuf, hbuf, qbuf, gbuf, zbuf, acc):
    adjoint_step(err, wa, level, codes, ebuf, hbuf, qbuf, gbuf, new_codes)
    synthesis(new_codes, ws, zbuf, acc, part)


def last_kernel(err, codes, out, parts, lbuf, cbuf, gacc, sem):
    copies = [pltpu.make_async_copy(codes.at[i], out.at[:, i], sem.at[i]) for i in range(ROWS)]
    for copy in copies:
        copy.start()
    correlation(err, codes, lbuf, cbuf, gacc, parts)
    for copy in copies:
        copy.wait()


def greet(peers):
    barrier = pltpu.get_barrier_semaphore()
    for peer in peers:
        pl.semaphore_signal(barrier, inc=1, device_id=peer, device_id_type=MESH)
    pl.semaphore_wait(barrier, len(peers))


def send(src, dst, sems, slot, peer):
    copy = pltpu.make_async_remote_copy(
        src_ref=src,
        dst_ref=dst,
        send_sem=sems.at[0, slot],
        recv_sem=sems.at[1, slot],
        device_id=peer,
        device_id_type=MESH,
    )
    copy.start()
    return copy


def wait_all(copies):
    for copy in copies:
        copy.wait_recv()
    for copy in copies:
        copy.wait_send()


def exchange_kernel(
    sizes, part, image, err, rbuf, piece, piece2, h1, msg, h2, field, s_rs, s_h1, s_h2, s_ag
):
    owners, rows, cols = sizes
    share = C // owners
    q, r, c = lax.axis_index("atom"), lax.axis_index("row"), lax.axis_index("col")
    others = [{"atom": lax.rem(q + d, owners)} for d in range(1, owners)]
    up, down = {"row": lax.rem(r + rows - 1, rows)}, {"row": lax.rem(r + 1, rows)}
    left, right = {"col": lax.rem(c + cols - 1, cols)}, {"col": lax.rem(c + 1, cols)}
    greet(others + [up, down, left, right])

    wait_all(
        [send(part.at[p["atom"]], rbuf.at[d], s_rs, d, p) for d, p in enumerate(others)]
    )
    total = part[q]
    for d in range(owners - 1):
        total = total + rbuf[d]
    total = total * SCALE
    piece[0:5] = total[0:5]
    piece[5:21] = total[5:21] - image[...]
    piece[21:SLOTS] = total[21:SLOTS]

    f_up, f_down = (r > 0).astype(F32), (r < rows - 1).astype(F32)
    f_left, f_right = (c > 0).astype(F32), (c < cols - 1).astype(F32)
    lane = lane_index(share)
    wait_all(
        [
            send(piece.at[17:26], h1.at[0], s_h1, 0, down),
            send(piece.at[0:9], h1.at[1], s_h1, 1, up),
        ]
    )
    piece2[0] = piece[0] + h1[0, 8] * f_up
    piece2[1:9] = piece[1:9] + h1[0, 0:8] * f_up
    piece2[9:17] = piece[9:17]
    piece2[17:25] = piece[17:25] + h1[1, 1:9] * f_down
    piece2[25] = piece[25] + jnp.where(lane < 64, h1[1, 0], 0.0) * f_down

    ends = (lane < 4) | (lane >= LANES - 4)
    low = lane % 8 < 4
    packed = [jnp.zeros((share, LANES), F32), jnp.zeros((share, LANES), F32)]
    for row in range(EXT):
        packed[row // 16] += roll(jnp.where(ends, piece2[row + 1], 0.0), 8 * (row % 16) + 4)
    rims = [piece2[0], piece2[SLOTS - 1]]
    for v in range(2):
        msg[0, v] = jnp.where(low, packed[v], rims[v])
        msg[1, v] = jnp.where(low, rims[v], packed[v])
    wait_all(
        [
            send(msg.at[0], h2.at[0], s_h2, 0, right),
            send(msg.at[1], h2.at[1], s_h2, 1, left),
        ]
    )
    inner = [None, None]
    for v in range(2):
        from_left, from_right = h2[0, v] * f_left, h2[1, v] * f_right
        rims[v] = rims[v] + jnp.where(low, from_left, from_right)
        inner[v] = jnp.where(low, from_right, from_left)
        rims[v] = rims[v] * jnp.where(low, f_left, f_right)
    for row in range(EXT):
        fix = roll(inner[row // 16], -(8 * (row % 16) + 4))
        value = piece2[row + 1] + jnp.where(ends, fix, 0.0)
        if row < 4:
            value = value * f_up
        if row >= EXT - 4:
            value = value * f_down
        field[row + 1] = value
    field[0] = rims[0] * jnp.where(lane < 32, f_up, 1.0)
    field[SLOTS - 1] = jnp.where(lane < 64, rims[1] * jnp.where(lane >= 32, f_down, 1.0), 0.0)

    copies = [send(field, err.at[q], s_ag, d, p) for d, p in enumerate(others)]
    err[q] = field[...]
    wait_all(copies)


def update_kernel(sizes, parts, atoms, velocity, new_atoms, new_velocity, half, total, chunks, s1, s2):
    rows, halves = sizes
    r, c = lax.axis_index("row"), lax.axis_index("col")
    core, z = lax.rem(c, 2), lax.div(c, 2)
    partner = {"col": 2 * z + 1 - core}
    others = []
    for dr in range(rows):
        for dz in range(halves):
            if dr + dz > 0:
                pr, pz = lax.rem(r + dr, rows), lax.rem(z + dz, halves)
                others.append((pr * halves + pz, {"row": pr, "col": 2 * pz + core}))
    greet([partner] + [p for _, p in others])
    wait_all([send(parts.at[1 - core], half, s1, 0, partner)])
    total[...] = parts[core] + half[...]
    wait_all([send(total.at[g], chunks.at[d], s2, d, p) for d, (g, p) in enumerate(others)])
    summed = total[r * halves + z]
    for d in range(len(others)):
        summed = summed + chunks[d]
    pixels = ROWS * LANES * rows * halves * 2
    fresh = MOMENTUM * velocity[...] + summed * (1.0 / pixels)
    stepped = atoms[...] - LEARN_RATE * fresh
    square = jnp.sum(jnp.sum(stepped * stepped, axis=0), axis=1, keepdims=True) * (1.0 / (T * T * C))
    new_velocity[...] = fresh
    new_atoms[...] = stepped * lax.rsqrt(square + EPSILON)[None]


def struct(shape, dtype=F32):
    return jax.ShapeDtypeStruct(shape, dtype)


def params(collective_id=None):
    if collective_id is None:
        return pltpu.CompilerParams(vmem_limit_bytes=60 << 20)
    return pltpu.CompilerParams(
        vmem_limit_bytes=60 << 20, collective_id=collective_id, has_side_effects=True
    )


def shards(hyper_image, warm_codes, dictionary, thresholds, velocity):
    owners, rows, cols = lax.axis_size("atom"), lax.axis_size("row"), lax.axis_size("col")
    share, owned, halves = C // owners, velocity.shape[0], cols // 2
    q = lax.axis_index("atom")

    hi = lax.reduce_precision(dictionary, 8, 7)
    lo = (dictionary - hi).astype(BF16)
    hi = hi.astype(BF16)
    triple = jnp.stack([hi, hi, lo])
    ws = triple.transpose(3, 4, 2, 0, 1).reshape(T * C, T * 3 * KL)
    ws = jnp.pad(ws, ((0, 0), (0, 3 * KL)))
    wa = triple[:, :, ::-1].transpose(3, 1, 2, 0, 4).reshape(T * KL, T * 3 * C)
    level = jnp.broadcast_to((ETA_CODE * thresholds)[:, None], (KL, LANES))
    image = lax.dynamic_slice_in_dim(hyper_image, q * share, share, 0).transpose(1, 0, 2)

    code_shape, part_shape = (ROWS, KL, LANES), (owners, SLOTS, share, LANES)
    synth_scratch = [
        pltpu.VMEM((10 * 3 * KL, 2 * LANES), BF16),
        pltpu.VMEM((8, C, LANES), F32),
    ]
    codes, part = pl.pallas_call(
        first_kernel,
        out_shape=(struct(code_shape), struct(part_shape)),
        in_specs=[ANY, VMEM],
        out_specs=(VMEM, VMEM),
        scratch_shapes=synth_scratch + [pltpu.SemaphoreType.DMA((ROWS,))],
        compiler_params=params(),
    )(warm_codes, ws)

    def exchange(part):
        piece = pltpu.VMEM((SLOTS, share, LANES), F32)
        return pl.pallas_call(
            functools.partial(exchange_kernel, (owners, rows, cols)),
            out_shape=struct(part_shape),
            in_specs=[VMEM, VMEM],
            out_specs=VMEM,
            scratch_shapes=[
                pltpu.VMEM((owners - 1, SLOTS, share, LANES), F32),
                piece,
                piece,
                pltpu.VMEM((2, 9, share, LANES), F32),
                pltpu.VMEM((2, 2, share, LANES), F32),
                pltpu.VMEM((2, 2, share, LANES), F32),
                piece,
                pltpu.SemaphoreType.DMA((2, owners - 1)),
                pltpu.SemaphoreType.DMA((2, 2)),
                pltpu.SemaphoreType.DMA((2, 2)),
                pltpu.SemaphoreType.DMA((2, owners - 1)),
            ],
            compiler_params=params(0),
        )(part, image)

    for _ in range(ITERS):
        err = exchange(part)
        codes, part = pl.pallas_call(
            step_kernel,
            out_shape=(struct(code_shape), struct(part_shape)),
            in_specs=[VMEM] * 5,
            out_specs=(VMEM, VMEM),
            scratch_shapes=[
                pltpu.VMEM((16 * 3 * C, 2 * LANES), BF16),
                pltpu.VMEM((T * 3 * C, LANES), BF16),
                pltpu.VMEM((T * KL, 2 * LANES), F32),
                pltpu.VMEM((KL, LANES), F32),
            ]
            + synth_scratch,
            compiler_params=params(),
        )(err, wa, ws, level, codes)
    err = exchange(part)

    new_codes, parts = pl.pallas_call(
        last_kernel,
        out_shape=(
            struct((KL, ROWS, LANES)),
            struct((2, rows * halves, T, owned, T * C)),
        ),
        in_specs=[VMEM, VMEM],
        out_specs=(ANY, VMEM),
        scratch_shapes=[
            pltpu.VMEM((T * C, EXT * 3 * LANES), BF16),
            pltpu.VMEM(((ROWS + 1) * KL, 6 * LANES), BF16),
            pltpu.VMEM((T * KL, T * C), F32),
            pltpu.SemaphoreType.DMA((ROWS,)),
        ],
        compiler_params=params(),
    )(err, codes)

    start = (lax.axis_index("row") * cols + lax.axis_index("col")) * owned

    def flat(block):
        return block.transpose(1, 0, 2, 3).reshape(T, owned, T * C)

    def unflat(block):
        return block.reshape(T, owned, T, C).transpose(1, 0, 2, 3)

    piece_shape = (T, owned, T * C)
    new_atoms, new_velocity = pl.pallas_call(
        functools.partial(update_kernel, (rows, halves)),
        out_shape=(struct(piece_shape), struct(piece_shape)),
        in_specs=[VMEM] * 3,
        out_specs=(VMEM, VMEM),
        scratch_shapes=[
            pltpu.VMEM((rows * halves,) + piece_shape, F32),
            pltpu.VMEM((rows * halves,) + piece_shape, F32),
            pltpu.VMEM((rows * halves - 1,) + piece_shape, F32),
            pltpu.SemaphoreType.DMA((2, 1)),
            pltpu.SemaphoreType.DMA((2, rows * halves - 1)),
        ],
        compiler_params=params(1),
    )(
        parts,
        flat(lax.dynamic_slice_in_dim(dictionary, start, owned, 0)),
        flat(velocity),
    )
    return new_codes, unflat(new_atoms), unflat(new_velocity)


def solution(mesh):
    in_specs = (
        P(None, "row", "col"),
        P("atom", "row", "col"),
        P("atom", None, None, None),
        P("atom"),
        P(("atom", "row", "col"), None, None, None),
    )
    out_specs = (
        P("atom", "row", "col"),
        P(("atom", "row", "col"), None, None, None),
        P(("atom", "row", "col"), None, None, None),
    )
    return jax.shard_map(shards, mesh=mesh, in_specs=in_specs, out_specs=out_specs, check_vma=False)
```

time: 858 us -> 154 us (0.18)
  waiting for transfers between devices: 396 us -> 0 us
  matrix products: 289 us -> 0 us
  Pallas kernels: 0 us -> 124 us
  starting transfers between devices: 70.9 us -> 0 us
  local copies, waits for them, and re-layouts: 58.8 us -> 24.5 us
  between operations: 15.2 us -> 0.79 us
  other arithmetic: 16.9 us -> 3.38 us
    psum x4 -> x0, waiting for transfers between devices: 341 us -> none  [the longest x3 193 us: residual_whole(): summed = lax.psum(forward_image(padded_codes, dictionary), 'atom')]
    dot_general x486 -> x0, matrix products: 289 us -> none  [the longest x243 132 us: forward_row_step(): jnp.einsum('kc,khw->chw', tap_row[:, offset_col, :], strip_rows[:, :, off...]
    pallas_call x0 -> x8, Pallas kernels: none -> 124 us  [the longest x3 79.5 us: exchange(): pl.pallas_call(functools.partial(exchange_kernel, (owners, rows, cols)),...]
    ppermute x20 -> x0, starting transfers between devices: 70.8 us -> none  [the longest x10 53.6 us: padded_2(): lax.ppermute(lax.slice_in_dim(block, block.shape[dim] - width, None, axis...]
    ppermute x20 -> x0, waiting for transfers between devices: 54.3 us -> none  [the longest x10 44.8 us: padded_2(): lax.ppermute(lax.slice_in_dim(block, 0, width, axis=dim), axis, backward)]
    squeeze x45 -> x0, local copies, waits for them, and re-layouts: 41.6 us -> none  [the longest x27 25 us: forward_row_step(): lax.dynamic_index_in_dim(dictionary, offset_row, 1, keepdims=False)]
    reshape x1 -> x7, local copies, waits for them, and re-layouts: 3.1 us -> 13.1 us  [the longest x2 6.08 us: shards(): wa = triple[:, :, ::-1].transpose(3, 1, 2, 0, 4).reshape(T * KL, T * 3 * C)]
  transfers between devices with their start and end apart: 24 -> 0, of which waited for: 19 -> 0; matrix products, arithmetic and copies ran while one was open for 1% -> 0% of each run, Pallas kernels for 0% -> 0%
where the time goes in v1:
time: 154 us; the launch traced here: 153 us
  Pallas kernels  124 us (81%)
  local copies, waits for them, and re-layouts  24.5 us (16%)
  other arithmetic  3.38 us (2%)
    pallas_call x3, Pallas kernels, exchange(): pl.pallas_call(functools.partial(exchange_kernel, (owners, rows, cols)),...  79.5 us
    pallas_call x2, Pallas kernels, shards(): pl.pallas_call(step_kernel, out_shape=(struct(code_shape), struct(part_sh...  17.1 us
    pallas_call x1, Pallas kernels, shards(): pl.pallas_call(functools.partial(update_kernel, (rows, halves)), out_shap...  14.4 us
    pallas_call x1, Pallas kernels, shards(): pl.pallas_call(last_kernel, out_shape=(struct((KL, ROWS, LANES)), struct(...  7.15 us
    pallas_call x1, Pallas kernels, shards(): pl.pallas_call(first_kernel, out_shape=(struct(code_shape), struct(part_s...  6.27 us
    reshape x2, local copies, waits for them, and re-layouts, shards(): wa = triple[:, :, ::-1].transpose(3, 1, 2, 0, 4).reshape(T * KL, T * 3 * C)  6.08 us
    another operation x2, other arithmetic, shards(): triple = jnp.stack([hi, hi, lo])  3.38 us
    transpose x2, local copies, waits for them, and re-layouts, shards(): wa = triple[:, :, ::-1].transpose(3, 1, 2, 0, 4).reshape(T * KL, T * 3 * C)  3.35 us

profile of v1, /device:TPU:1, one launch (start us, length us, event | category | flops | bytes accessed | tf_op | source)
XLA Modules:
  0.0 153.1 jit_solution(16782341392968096327)
XLA Ops:
  0.6 0.0 copy-start
  0.7 0.9 copy-done
  1.6 0.6 copy.27
  2.2 1.5 %fusion.2 = (bf16[1,64,9,9,32]{1,4,3,2,0:T(8,128)(2,1)S(1)}, bf16[1,64,9,9,32]{1,4,3,2,0:T(8,128)(2,1)S(1)}) fusion(f32[64,9,9,32]{0,3,2,1:T(8,128)} %param.7), kind=kLoop, calls=%fused_computation.6 | loop fusion | flops 663552 | bytes 1327104 | tf_op jit(solution)/shard_map/stack | solution.py:370
  3.8 1.8 %pad_maximum_fusion = (bf16[3,64,9,9,32]{1,4,3,2,0:T(8,128)(2,1)}, bf16[9,32,9,3,64]{4,1,0,2,3:T(8,128)(2,1)S(1)}) fusion(bf16[1,64,9,9,32]{1,4,3,2,0:T(8,128)(2,1)S(1)} %get-tuple-element.29, bf16[1,64,9,9,32]{1,4,3,2,0:T(8,128)(2,1)S(1)} %get-tuple-element.28), kind=kLoop, calls=%fused_computation | loop fusion | flops 995328 | bytes 2654208 | tf_op jit(solution)/shard_map/stack | solution.py:370
  5.6 1.4 copy.15
  7.0 3.3 %reshape.25 = bf16[288,1728]{1,0:T(8,128)(2,1)} reshape(bf16[9,32,9,3,64]{4,3,2,1,0:T(4,128)(2,1)S(1)} %copy.15) | data formatting | bytes 1990656 | tf_op jit(solution)/shard_map/reshape | solution.py:371
  10.2 0.0 copy-start.1
  10.2 2.5 %pad.4.ws = bf16[288,1920]{1,0:T(8,128)(2,1)} pad(bf16[288,1728]{1,0:T(8,128)(2,1)} %reshape.25, bf16[]{:T(256)} %constant.6.clone.1), padding=0_0x0_192 | pad | bytes 2101250 | tf_op jit(solution)/shard_map/jit(_pad)/pad | solution.py:372
  12.7 6.3 %shard_map.76 = (f32[16,64,128]{2,1,0:T(8,128)}, f32[8,26,4,128]{3,2,1,0:T(4,128)}) custom-call(f32[64,16,128]{2,1,0:T(8,128)} %warm.1, bf16[288,1920]{1,0:T(8,128)(2,1)} %pad.4.ws), custom_call_target="tpu_custom_call" | custom-call | tf_op jit(solution)/shard_map/pallas_call | solution.py:382
  19.0 30.0 %shard_map.77.err = f32[8,26,4,128]{3,2,1,0:T(4,128)} custom-call(f32[8,26,4,128]{3,2,1,0:T(4,128)} %get-tuple-element.13.part, f32[16,4,128]{2,1,0:T(4,128)} %bitcast.22), custom_call_target="tpu_custom_call" | custom-call | tf_op jit(solution)/shard_map/pallas_call | solution.py:393
  49.0 0.0 copy-done.1
  49.0 0.3 reverse_bitcast_fusion
  49.3 3.0 %copy.17 = bf16[9,64,9,3,32]{1,0,4,3,2:T(8,128)(2,1)} copy(bf16[9,64,9,3,32]{1,4,0,2,3:T(8,128)(2,1)S(1)} %reverse_bitcast_fusion) | data formatting | bytes 1990656 | tf_op jit(solution)/shard_map/transpose | solution.py:373
  52.3 4.4 %reshape.26 = bf16[576,864]{0,1:T(8,128)(2,1)S(1)} reshape(bf16[9,64,9,3,32]{1,0,4,3,2:T(8,128)(2,1)} %copy.17) | data formatting | bytes 1990656 | tf_op jit(solution)/shard_map/reshape | solution.py:373
  56.7 0.0 copy-start.4
  56.7 1.7 %copy.18.wa = bf16[576,864]{1,0:T(8,128)(2,1)} copy(bf16[576,864]{0,1:T(8,128)(2,1)S(1)} %reshape.26) | data formatting | bytes 1990656 | tf_op jit(solution)/shard_map/reshape | solution.py:373
  58.4 0.0 copy-done.4
  58.4 0.7 broadcast_in_dim.2.level
  59.1 8.5 %shard_map.78 = (f32[16,64,128]{2,1,0:T(8,128)}, f32[8,26,4,128]{3,2,1,0:T(4,128)}) custom-call(f32[8,26,4,128]{3,2,1,0:T(4,128)} %shard_map.77.err, bf16[576,864]{1,0:T(8,128)(2,1)} %copy.18.wa, bf16[288,1920]{1,0:T(8,128)(2,1)} %pad.4.ws, f32[64,128]{1,0:T(8,128)} %broadcast_in_dim.2.level, f32[16,64,128]{2,1,0:T(8,128)} %get-tuple-element.14.codes), custom_call_target="tpu_custom_call" | custom-call | tf_op jit(solution)/shard_map/pallas_call | solution.py:416
  67.6 24.1 %shard_map.79.err = f32[8,26,4,128]{3,2,1,0:T(4,128)} custom-call(f32[8,26,4,128]{3,2,1,0:T(4,128)} %get-tuple-element.15.part, f32[16,4,128]{2,1,0:T(4,128)} %bitcast.23), custom_call_target="tpu_custom_call" | custom-call | tf_op jit(solution)/shard_map/pallas_call | solution.py:393
  91.7 0.0 copy-start.2
  91.7 8.6 %shard_map.80 = (f32[16,64,128]{2,1,0:T(8,128)}, f32[8,26,4,128]{3,2,1,0:T(4,128)}) custom-call(f32[8,26,4,128]{3,2,1,0:T(4,128)} %shard_map.79.err, bf16[576,864]{1,0:T(8,128)(2,1)} %copy.18.wa, bf16[288,1920]{1,0:T(8,128)(2,1)} %pad.4.ws, f32[64,128]{1,0:T(8,128)} %broadcast_in_dim.2.level, f32[16,64,128]{2,1,0:T(8,128)} %get-tuple-element.16.codes), custom_call_target="tpu_custom_call" | custom-call | tf_op jit(solution)/shard_map/pallas_call | solution.py:416
  100.4 25.5 %shard_map.81.err = f32[8,26,4,128]{3,2,1,0:T(4,128)} custom-call(f32[8,26,4,128]{3,2,1,0:T(4,128)} %get-tuple-element.17.part, f32[16,4,128]{2,1,0:T(4,128)} %bitcast.24), custom_call_target="tpu_custom_call" | custom-call | tf_op jit(solution)/shard_map/pallas_call | solution.py:393
  125.8 7.2 %shard_map.82 = (f32[64,16,128]{2,1,0:T(8,128)}, f32[2,8,9,4,288]{4,3,2,1,0:T(4,128)}) custom-call(f32[8,26,4,128]{3,2,1,0:T(4,128)} %shard_map.81.err, f32[16,64,128]{2,1,0:T(8,128)} %get-tuple-element.18.codes), custom_call_target="tpu_custom_call" | custom-call | tf_op jit(solution)/shard_map/pallas_call | solution.py:432
  133.0 0.0 copy-done.2
  133.0 0.0 copy-start.3
  133.0 0.4 constant_dynamic-slice_fusion
  133.4 1.2 copy.24.atoms
  134.6 0.0 copy-done.3
  134.6 0.7 reshape.28.velocity
  135.4 14.4 %shard_map.83 = (f32[9,4,288]{2,1,0:T(4,128)}, f32[9,4,288]{2,1,0:T(4,128)}) custom-call(f32[2,8,9,4,288]{4,3,2,1,0:T(4,128)} %get-tuple-element.20.parts, f32[9,4,288]{2,1,0:T(4,128)} %copy.24.atoms, f32[9,4,288]{2,1,0:T(4,128)} %reshape.28.velocity), custom_call_target="tpu_custom_call" | custom-call | tf_op jit(solution)/shard_map/pallas_call | solution.py:458
  149.8 0.9 reshape.29
  150.7 0.7 copy.22
  151.5 0.9 reshape.30
  152.4 0.7 copy.23
  (3 shorter events, 0.0 us)
Async XLA Ops:
  0.6 1.0 copy-start
  10.2 38.7 %copy-start.1 = (bf16[3,64,9,9,32]{1,4,3,2,0:T(8,128)(2,1)S(1)}, bf16[3,64,9,9,32]{1,4,3,2,0:T(8,128)(2,1)}, u32[]{:S(2)}) copy-start(bf16[3,64,9,9,32]{1,4,3,2,0:T(8,128)(2,1)} %get-tuple-element.26) | copy-start | bytes 2985988
  56.7 1.7 %copy-start.4 = (f32[64]{0:T(128)S(1)}, f32[64]{0:T(128)}, u32[]{:S(2)}) copy-start(f32[64]{0:T(128)} %param.8) | copy-start | bytes 772
  91.7 41.3 %copy-start.2 = (f32[64,9,9,32]{0,3,2,1:T(8,128)S(1)}, f32[64,9,9,32]{0,3,2,1:T(8,128)}, u32[]{:S(2)}) copy-start(f32[64,9,9,32]{0,3,2,1:T(8,128)} %param.7) | copy-start | bytes 1990660
  133.0 1.6 %copy-start.3 = (f32[4,9,9,32]{3,0,2,1:T(4,128)S(1)}, f32[4,9,9,32]{3,0,2,1:T(4,128)}, u32[]{:S(2)}) copy-start(f32[4,9,9,32]{3,0,2,1:T(4,128)} %param.9) | copy-start | bytes 124420

commit v2 on v1

v2 whole, which is shorter than its diff:
```python
import functools
import math

import jax
import jax.numpy as jnp
from jax import lax
from jax.experimental import pallas as pl
from jax.experimental.pallas import tpu as pltpu
from jax.sharding import PartitionSpec as P

ITERS = 2
ETA_CODE = 0.05
MOMENTUM = 0.9
LEARN_RATE = 200.0
EPSILON = 1e-06

F32 = jnp.float32
BF16 = jnp.bfloat16
MESH = pl.DeviceIdType.MESH
VMEM = pl.BlockSpec(memory_space=pltpu.VMEM)
ANY = pl.BlockSpec(memory_space=pl.ANY)

C = 32
T = 9
KL = 64
ROWS = 16
LANES = 128
EXT = ROWS + 8
SLOTS = EXT + 2
SCALE = 1.0 / math.sqrt(T * T * C)


def split(x):
    hi = x.astype(BF16)
    return hi, (x - hi.astype(F32)).astype(BF16)


def lane_index(rows):
    return lax.broadcasted_iota(jnp.int32, (rows, LANES), 1)


def roll(x, shift):
    return pltpu.roll(x, shift % LANES, 1) if shift % LANES else x


def inside(lane, shift):
    return lane >= shift if shift > 0 else lane < LANES + shift


def synthesis(codes, ws, zbuf, acc, part):
    owners = part.shape[0]
    share = C // owners
    lane = lane_index(C)
    zero_rows = jnp.zeros((3 * KL, 2 * LANES), BF16)
    zbuf[0 : 3 * KL] = zero_rows
    zbuf[9 * 3 * KL : 10 * 3 * KL] = zero_rows
    for t in range(8):
        hi, lo = split(jnp.concatenate([codes[t], codes[t + 8]], axis=1))
        base = (t + 1) * 3 * KL
        zbuf[base : base + KL] = hi
        zbuf[base + KL : base + 2 * KL] = lo
        zbuf[base + 2 * KL : base + 3 * KL] = hi
    rims = [jnp.zeros((C, LANES), F32), jnp.zeros((C, LANES), F32)]

    def put(slot, row):
        for q in range(owners):
            part[q, slot] = row[q * share : (q + 1) * share]

    for ho in range(16):
        first, last = max(0, 8 - ho) // 2, min(8, 15 - ho) // 2
        depth = (last - first + 1) * 6 * KL
        start = (2 * first + ho - 7) * 3 * KL
        taps = jnp.dot(
            ws[:, first * 6 * KL : first * 6 * KL + depth],
            zbuf[start : start + depth],
            preferred_element_type=F32,
        )
        for half in range(2):
            main = jnp.zeros((C, LANES), F32)
            rim = jnp.zeros((C, LANES), F32)
            for b in range(T):
                moved = roll(taps[b * C : (b + 1) * C, half * LANES : (half + 1) * LANES], 4 - b)
                if b == 4:
                    main = main + moved
                else:
                    keep = inside(lane, 4 - b)
                    main = main + jnp.where(keep, moved, 0.0)
                    rim = rim + jnp.where(keep, 0.0, moved)
            row = ho + 8 * half
            rims[row // 16] = rims[row // 16] + roll(rim, 8 * (row % 16) + 4)
            if half == 0 and ho >= 8:
                main = main + acc[ho - 8]
            if half == 1 and ho < 8:
                acc[ho] = main
            else:
                put(row + 1, main)
    put(0, rims[0])
    put(SLOTS - 1, rims[1])


def gathered(err, slot):
    return jnp.concatenate([err[q, slot] for q in range(err.shape[0])], axis=0)


def adjoint_step(err, wa, level, codes, ebuf, hbuf, qbuf, gbuf):
    wide = 3 * C
    lane_c = lane_index(C)
    lane = lane_index(KL)
    spot = lane % 8
    for row in range(EXT):
        hi, lo = split(gathered(err, row + 1))
        for t, side in ((row, 0), (row - 8, 1)):
            if 0 <= t < 16:
                cols = slice(side * LANES, (side + 1) * LANES)
                ebuf[t * wide : t * wide + C, cols] = hi
                ebuf[t * wide + C : t * wide + 2 * C, cols] = lo
                ebuf[t * wide + 2 * C : t * wide + 3 * C, cols] = hi
    rims = [gathered(err, 0), gathered(err, SLOTS - 1)]
    for t in range(T):
        hi, lo = split(
            jnp.where(lane_c < LANES - 8 * t, roll(rims[0], -8 * t), roll(rims[1], -8 * t))
        )
        hbuf[t * wide : t * wide + C] = hi
        hbuf[t * wide + C : t * wide + 2 * C] = lo
        hbuf[t * wide + 2 * C : t * wide + 3 * C] = hi
    qbuf[:, 0:LANES] = jnp.dot(wa[:, 0 : T * wide], hbuf[...], preferred_element_type=F32)
    edge = jnp.zeros((KL, LANES), F32)
    for b in range(T):
        s = b - 4
        if s == 0:
            continue
        keep = (spot >= 4) & (spot < 4 + s) if s > 0 else (spot < 4) & (spot >= 4 + s)
        edge = edge + jnp.where(keep, roll(qbuf[b * KL : (b + 1) * KL, 0:LANES], s), 0.0)
    gbuf[...] = edge
    ends = (lane < 4) | (lane >= LANES - 4)
    bound = level[...]
    for i in range(8):
        qbuf[...] = jnp.dot(
            wa[:, 0 : T * wide], ebuf[i * wide : (i + T) * wide], preferred_element_type=F32
        )
        for half in range(2):
            row = i + 8 * half
            total = jnp.where(ends, roll(gbuf[...], -(8 * row + 4)), 0.0)
            for b in range(T):
                moved = roll(qbuf[b * KL : (b + 1) * KL, half * LANES : (half + 1) * LANES], b - 4)
                if b != 4:
                    moved = jnp.where(inside(lane, b - 4), moved, 0.0)
                total = total + moved
            shifted = codes[row] - (ETA_CODE * SCALE) * total
            codes[row] = shifted - jnp.clip(shifted, -bound, bound)


def correlation(err, codes, lbuf, cbuf, gacc, parts):
    lane = lane_index(C)
    rims = [gathered(err, 0), gathered(err, SLOTS - 1)]
    for row in range(EXT):
        main = gathered(err, row + 1)
        rim = roll(rims[row // 16], -(8 * (row % 16) + 4))
        for b in range(T):
            s = b - 4
            if s > 0:
                field = jnp.where(lane >= LANES - s, rim, main)
            elif s < 0:
                field = jnp.where(lane < -s, rim, main)
            else:
                field = main
            hi, lo = split(roll(field, s))
            at = row * 3 * LANES
            lbuf[b * C : (b + 1) * C, at : at + LANES] = hi
            lbuf[b * C : (b + 1) * C, at + LANES : at + 2 * LANES] = hi
            lbuf[b * C : (b + 1) * C, at + 2 * LANES : at + 3 * LANES] = lo
    none = jnp.zeros((KL, 3 * LANES), BF16)
    cbuf[0:KL, 0 : 3 * LANES] = none
    cbuf[ROWS * KL : (ROWS + 1) * KL, 3 * LANES : 6 * LANES] = none
    for i in range(ROWS):
        hi, lo = split(codes[i])
        for at, base in (((i + 1) * KL, 0), (i * KL, 3 * LANES)):
            cbuf[at : at + KL, base : base + LANES] = hi
            cbuf[at : at + KL, base + LANES : base + 2 * LANES] = lo
            cbuf[at : at + KL, base + 2 * LANES : base + 3 * LANES] = hi
    gacc[...] = jnp.zeros_like(gacc)
    for row in range(0, EXT, 2):
        low, high = max(row - 8, -1), min(row, ROWS - 1)
        a = low - row + 8
        count = (high - low + 1) * KL
        gacc[a * KL : a * KL + count] += lax.dot_general(
            cbuf[(low + 1) * KL : (low + 1) * KL + count],
            lbuf[:, row * 3 * LANES : (row + 2) * 3 * LANES],
            (((1,), (1,)), ((), ())),
            preferred_element_type=F32,
        )
    groups, share = parts.shape[1], parts.shape[3]
    for core in range(2):
        for g in range(groups):
            for a in range(T):
                at = a * KL + (2 * g + core) * share
                parts[core, g, a] = gacc[at : at + share]


def synthesis_weights(atoms, ws):
    for a in range(0, T + 1, 2):
        pairs = []
        for t in (a, a + 1):
            if t < T:
                field = jnp.concatenate([atoms[t, b] for b in range(T)], axis=0)
                hi, lo = split(field)
                pairs += [hi.astype(F32), hi.astype(F32), lo.astype(F32)]
            else:
                pairs += [jnp.zeros((T * C, KL), F32)] * 3
        for n in range(3):
            lanes = slice(a * 3 * KL + n * LANES, a * 3 * KL + (n + 1) * LANES)
            ws[:, lanes] = jnp.concatenate(pairs[2 * n : 2 * n + 2], axis=1).astype(BF16)


def adjoint_weights(atoms, flip, wa):
    depth = flip.shape[0]
    flip[T * 3 * C : depth] = jnp.zeros((depth - T * 3 * C, flip.shape[1]), F32)
    flip[:, T * KL :] = jnp.zeros((depth, flip.shape[1] - T * KL), F32)
    for a in range(T):
        at = (T - 1 - a) * 3 * C
        for b in range(0, T, 2):
            cols = slice(b * KL, min(b + 2, T) * KL)
            field = atoms[a, b]
            if b + 1 < T:
                field = jnp.concatenate([field, atoms[a, b + 1]], axis=1)
            hi, lo = split(field)
            flip[at : at + C, cols] = hi.astype(F32)
            flip[at + C : at + 2 * C, cols] = hi.astype(F32)
            flip[at + 2 * C : at + 3 * C, cols] = lo.astype(F32)
    for m in range(0, flip.shape[1], LANES):
        rows = min(LANES, T * KL - m)
        for n in range(0, depth, LANES):
            turned = jnp.transpose(flip[n : n + LANES, m : m + LANES])
            wa[m : m + rows, n : n + LANES] = turned[:rows].astype(BF16)


def owned_atoms(atoms, start, share, own):
    row = lax.broadcasted_iota(jnp.int32, (16, KL), 0)
    col = lax.broadcasted_iota(jnp.int32, (16, KL), 1)
    pick = jnp.where(col == row + start, 1.0, 0.0).astype(BF16)
    for a in range(T):
        field = jnp.concatenate([atoms[a, b] for b in range(T)], axis=0)
        hi, rest = field.astype(BF16), None
        rest = field - hi.astype(F32)
        mid = rest.astype(BF16)
        low = (rest - mid.astype(F32)).astype(BF16)
        total = None
        for piece in (hi, mid, low):
            part = lax.dot_general(
                pick, piece, (((1,), (1,)), ((), ())), preferred_element_type=F32
            )
            total = part if total is None else total + part
        own[a] = total[:share]


def greet(peers):
    barrier = pltpu.get_barrier_semaphore()
    for peer in peers:
        pl.semaphore_signal(barrier, inc=1, device_id=peer, device_id_type=MESH)


def greeted(peers):
    pl.semaphore_wait(pltpu.get_barrier_semaphore(), len(peers))


def send(src, dst, sems, slot, peer):
    copy = pltpu.make_async_remote_copy(
        src_ref=src,
        dst_ref=dst,
        send_sem=sems.at[0, slot],
        recv_sem=sems.at[1, slot],
        device_id=peer,
        device_id_type=MESH,
    )
    copy.start()
    return copy


def wait_all(copies):
    for copy in copies:
        copy.wait_recv()
    for copy in copies:
        copy.wait_send()


class Grid:
    def __init__(self, owners, rows, cols):
        self.owners, self.rows, self.cols, self.halves = owners, rows, cols, cols // 2
        self.q, self.r, self.c = (lax.axis_index(n) for n in ("atom", "row", "col"))
        q, r, c = self.q, self.r, self.c
        self.core, self.z = lax.rem(c, 2), lax.div(c, 2)
        self.peers = [{"atom": lax.rem(q + d, owners)} for d in range(1, owners)]
        self.up, self.down = {"row": lax.rem(r + rows - 1, rows)}, {"row": lax.rem(r + 1, rows)}
        self.left, self.right = {"col": lax.rem(c + cols - 1, cols)}, {"col": lax.rem(c + 1, cols)}
        self.partner = {"col": 2 * self.z + 1 - self.core}
        self.blocks = []
        for dr in range(rows):
            for dz in range(self.halves):
                if dr + dz > 0:
                    pr, pz = lax.rem(r + dr, rows), lax.rem(self.z + dz, self.halves)
                    place = {"row": pr, "col": 2 * pz + self.core}
                    self.blocks.append((pr * self.halves + pz, place))
        self.everyone = self.peers + [self.left, self.right] + [p for _, p in self.blocks]


def exchange(grid, part, image, err, rbuf, piece, piece2, h1, msg, h2, field, sems, meanwhile):
    s_rs, s_h1, s_h2, s_ag = sems
    owners, rows, cols, share = grid.owners, grid.rows, grid.cols, C // grid.owners
    copies = [send(part.at[p["atom"]], rbuf.at[d], s_rs, d, p) for d, p in enumerate(grid.peers)]
    meanwhile()
    wait_all(copies)
    total = part[grid.q]
    for d in range(owners - 1):
        total = total + rbuf[d]
    total = total * SCALE
    piece[0:5] = total[0:5]
    piece[5:21] = total[5:21] - image[...]
    piece[21:SLOTS] = total[21:SLOTS]

    f_up, f_down = (grid.r > 0).astype(F32), (grid.r < rows - 1).astype(F32)
    f_left, f_right = (grid.c > 0).astype(F32), (grid.c < cols - 1).astype(F32)
    lane = lane_index(share)
    wait_all(
        [
            send(piece.at[17:26], h1.at[0], s_h1, 0, grid.down),
            send(piece.at[0:9], h1.at[1], s_h1, 1, grid.up),
        ]
    )
    piece2[0] = piece[0] + h1[0, 8] * f_up
    piece2[1:9] = piece[1:9] + h1[0, 0:8] * f_up
    piece2[9:17] = piece[9:17]
    piece2[17:25] = piece[17:25] + h1[1, 1:9] * f_down
    piece2[25] = piece[25] + jnp.where(lane < 64, h1[1, 0], 0.0) * f_down

    ends = (lane < 4) | (lane >= LANES - 4)
    low = lane % 8 < 4
    packed = [jnp.zeros((share, LANES), F32), jnp.zeros((share, LANES), F32)]
    for row in range(EXT):
        packed[row // 16] += roll(jnp.where(ends, piece2[row + 1], 0.0), 8 * (row % 16) + 4)
    rims = [piece2[0], piece2[SLOTS - 1]]
    for v in range(2):
        msg[0, v] = jnp.where(low, packed[v], rims[v])
        msg[1, v] = jnp.where(low, rims[v], packed[v])
    wait_all(
        [
            send(msg.at[0], h2.at[0], s_h2, 0, grid.right),
            send(msg.at[1], h2.at[1], s_h2, 1, grid.left),
        ]
    )
    inner = [None, None]
    for v in range(2):
        from_left, from_right = h2[0, v] * f_left, h2[1, v] * f_right
        rims[v] = rims[v] + jnp.where(low, from_left, from_right)
        inner[v] = jnp.where(low, from_right, from_left)
        rims[v] = rims[v] * jnp.where(low, f_left, f_right)
    for row in range(EXT):
        fix = roll(inner[row // 16], -(8 * (row % 16) + 4))
        value = piece2[row + 1] + jnp.where(ends, fix, 0.0)
        if row < 4:
            value = value * f_up
        if row >= EXT - 4:
            value = value * f_down
        field[row + 1] = value
    field[0] = rims[0] * jnp.where(lane < 32, f_up, 1.0)
    field[SLOTS - 1] = jnp.where(lane < 64, rims[1] * jnp.where(lane >= 32, f_down, 1.0), 0.0)

    copies = [send(field, err.at[grid.q], s_ag, d, p) for d, p in enumerate(grid.peers)]
    err[grid.q] = field[...]
    wait_all(copies)


def update(grid, parts, own, velocity, new_atoms, new_velocity, half, total, chunks, s1, s2):
    wait_all([send(parts.at[1 - grid.core], half, s1, 0, grid.partner)])
    total[...] = parts[grid.core] + half[...]
    wait_all([send(total.at[g], chunks.at[d], s2, d, p) for d, (g, p) in enumerate(grid.blocks)])
    summed = total[grid.r * grid.halves + grid.z]
    for d in range(len(grid.blocks)):
        summed = summed + chunks[d]
    pixels = ROWS * LANES * grid.rows * grid.cols
    summed = summed * (1.0 / pixels)
    square = None
    for b in range(T):
        cols = slice(b * C, (b + 1) * C)
        fresh = MOMENTUM * velocity[:, b] + summed[:, :, cols]
        stepped = own[:, :, cols] - LEARN_RATE * fresh
        new_velocity[:, b] = fresh
        new_atoms[:, b] = stepped
        term = jnp.sum(stepped * stepped, axis=0)
        square = term if square is None else square + term
    square = jnp.sum(square, axis=1, keepdims=True) * (1.0 / (T * T * C))
    gain = lax.rsqrt(square + EPSILON)
    for b in range(T):
        new_atoms[:, b] = new_atoms[:, b] * gain[None]


def kernel(sizes, names, image, warm, atoms, limits, velocity, new_codes, new_atoms, new_velocity, *scratch):
    u = dict(zip(names, scratch))
    grid = Grid(*sizes)
    share, owned = C // grid.owners, velocity.shape[2]
    greet(grid.everyone)
    codes = u["codes"]
    loads = [pltpu.make_async_copy(atoms, u["atoms"], u["s_in"].at[0])]
    for i in range(ROWS):
        loads.append(pltpu.make_async_copy(warm.at[:, i], codes.at[i], u["s_in"].at[1 + i]))
    for i in range(ROWS):
        bands = image.at[pl.ds(grid.q * share, share), i]
        loads.append(pltpu.make_async_copy(bands, u["image"].at[i], u["s_in"].at[1 + ROWS + i]))
    for load in loads:
        load.start()
    diagonal = lax.broadcasted_iota(jnp.int32, (KL, KL), 0) == lax.broadcasted_iota(
        jnp.int32, (KL, KL), 1
    )
    column = jnp.sum(jnp.where(diagonal, limits[...], 0.0), axis=1, keepdims=True)
    u["level"][...] = jnp.broadcast_to(ETA_CODE * column, (KL, LANES))
    loads[0].wait()
    synthesis_weights(u["atoms"], u["ws"])
    for load in loads[1:]:
        load.wait()
    synthesis(codes, u["ws"], u["zbuf"], u["acc"], u["part"])

    def meet(n, meanwhile):
        exchange(
            grid,
            u["part"],
            u["image"],
            u["err"].at[n],
            u["rbuf"].at[n],
            u["piece"],
            u["piece2"],
            u["h1"].at[n],
            u["msg"],
            u["h2"].at[n],
            u["field"],
            [u[s].at[n] for s in ("s_rs", "s_h1", "s_h2", "s_ag")],
            meanwhile,
        )

    def prepare():
        adjoint_weights(u["atoms"], u["flip"], u["wa"])
        start = (grid.r * grid.cols + grid.c) * owned
        owned_atoms(u["atoms"], start, owned, u["own"])

    greeted(grid.everyone)
    meet(0, prepare)

    def one(n, carry):
        buffers = [u[s] for s in ("ebuf", "hbuf", "qbuf", "gbuf")]
        adjoint_step(u["err"].at[n - 1], u["wa"], u["level"], codes, *buffers)
        synthesis(codes, u["ws"], u["zbuf"], u["acc"], u["part"])
        meet(n, lambda: None)
        return carry

    lax.fori_loop(1, ITERS + 1, one, 0)
    stores = [
        pltpu.make_async_copy(codes.at[i], new_codes.at[:, i], u["s_in"].at[i]) for i in range(ROWS)
    ]
    for store in stores:
        store.start()
    correlation(u["err"].at[ITERS], codes, u["lbuf"], u["cbuf"], u["gacc"], u["parts"])
    buffers = [u[s] for s in ("half", "total", "chunks", "s_core", "s_block")]
    update(grid, u["parts"], u["own"], velocity, new_atoms, new_velocity, *buffers)
    for store in stores:
        store.wait()


def struct(shape, dtype=F32):
    return jax.ShapeDtypeStruct(shape, dtype)


def shards(hyper_image, warm_codes, dictionary, thresholds, velocity):
    owners, rows, cols = lax.axis_size("atom"), lax.axis_size("row"), lax.axis_size("col")
    share, owned, halves = C // owners, velocity.shape[0], cols // 2
    rounds, groups = ITERS + 1, rows * halves
    piece = pltpu.VMEM((SLOTS, share, LANES), F32)
    chunk = (T, owned, T * C)
    sems = pltpu.SemaphoreType.DMA
    scratch = {
        "codes": pltpu.VMEM((ROWS, KL, LANES), F32),
        "atoms": pltpu.VMEM((T, T, C, KL), F32),
        "image": pltpu.VMEM((ROWS, share, LANES), F32),
        "level": pltpu.VMEM((KL, LANES), F32),
        "ws": pltpu.VMEM((T * C, (T + 1) * 3 * KL), BF16),
        "flip": pltpu.VMEM((7 * LANES, 5 * LANES), F32),
        "wa": pltpu.VMEM((T * KL, 7 * LANES), BF16),
        "own": pltpu.VMEM(chunk, F32),
        "zbuf": pltpu.VMEM((10 * 3 * KL, 2 * LANES), BF16),
        "acc": pltpu.VMEM((8, C, LANES), F32),
        "part": pltpu.VMEM((owners, SLOTS, share, LANES), F32),
        "err": pltpu.VMEM((rounds, owners, SLOTS, share, LANES), F32),
        "rbuf": pltpu.VMEM((rounds, owners - 1, SLOTS, share, LANES), F32),
        "piece": piece,
        "piece2": piece,
        "h1": pltpu.VMEM((rounds, 2, 9, share, LANES), F32),
        "msg": pltpu.VMEM((2, 2, share, LANES), F32),
        "h2": pltpu.VMEM((rounds, 2, 2, share, LANES), F32),
        "field": piece,
        "ebuf": pltpu.VMEM((16 * 3 * C, 2 * LANES), BF16),
        "hbuf": pltpu.VMEM((T * 3 * C, LANES), BF16),
        "qbuf": pltpu.VMEM((T * KL, 2 * LANES), F32),
        "gbuf": pltpu.VMEM((KL, LANES), F32),
        "lbuf": pltpu.VMEM((T * C, EXT * 3 * LANES), BF16),
        "cbuf": pltpu.VMEM(((ROWS + 1) * KL, 6 * LANES), BF16),
        "gacc": pltpu.VMEM((T * KL, T * C), F32),
        "parts": pltpu.VMEM((2, groups) + chunk, F32),
        "half": pltpu.VMEM((groups,) + chunk, F32),
        "total": pltpu.VMEM((groups,) + chunk, F32),
        "chunks": pltpu.VMEM((groups - 1,) + chunk, F32),
        "s_in": sems((1 + 2 * ROWS,)),
        "s_rs": sems((rounds, 2, owners - 1)),
        "s_h1": sems((rounds, 2, 2)),
        "s_h2": sems((rounds, 2, 2)),
        "s_ag": sems((rounds, 2, owners - 1)),
        "s_core": sems((2, 1)),
        "s_block": sems((2, groups - 1)),
    }
    natural = (T, T, owned, C)
    new_codes, new_atoms, new_velocity = pl.pallas_call(
        functools.partial(kernel, (owners, rows, cols), tuple(scratch)),
        out_shape=(struct((KL, ROWS, LANES)), struct(natural), struct(natural)),
        in_specs=[ANY, ANY, ANY, VMEM, VMEM],
        out_specs=(ANY, VMEM, VMEM),
        scratch_shapes=list(scratch.values()),
        compiler_params=pltpu.CompilerParams(
            vmem_limit_bytes=60 << 20, collective_id=0, has_side_effects=True
        ),
    )(
        hyper_image,
        warm_codes,
        dictionary.transpose(1, 2, 3, 0),
        thresholds.reshape(1, KL),
        velocity.transpose(1, 2, 0, 3),
    )
    return new_codes, new_atoms.transpose(2, 0, 1, 3), new_velocity.transpose(2, 0, 1, 3)


def solution(mesh):
    in_specs = (
        P(None, "row", "col"),
        P("atom", "row", "col"),
        P("atom", None, None, None),
        P("atom"),
        P(("atom", "row", "col"), None, None, None),
    )
    out_specs = (
        P("atom", "row", "col"),
        P(("atom", "row", "col"), None, None, None),
        P(("atom", "row", "col"), None, None, None),
    )
    return jax.shard_map(shards, mesh=mesh, in_specs=in_specs, out_specs=out_specs, check_vma=False)
```

time: 154 us -> 106 us (0.69)
  Pallas kernels: 124 us -> 101 us
  local copies, waits for them, and re-layouts: 24.5 us -> 4.17 us
  other arithmetic: 3.38 us -> 0 us
    pallas_call x8 -> x1, Pallas kernels: 124 us -> 101 us  [shards(): pl.pallas_call(functools.partial(kernel, (owners, rows, cols), tuple(scra...]
    reshape x7 -> x0, local copies, waits for them, and re-layouts: 13.1 us -> none  [the longest x2 6.08 us: shards(): wa = triple[:, :, ::-1].transpose(3, 1, 2, 0, 4).reshape(T * KL, T * 3 * C)]
    transpose x4 -> x0, local copies, waits for them, and re-layouts: 4.74 us -> none  [the longest x2 3.35 us: shards(): wa = triple[:, :, ::-1].transpose(3, 1, 2, 0, 4).reshape(T * KL, T * 3 * C)]
    another operation x2 -> x0, other arithmetic: 3.38 us -> none  [shards(): triple = jnp.stack([hi, hi, lo])]
    pad x1 -> x0, local copies, waits for them, and re-layouts: 2.46 us -> none  [shards(): ws = jnp.pad(ws, ((0, 0), (0, 3 * KL)))]
    unnamed x13 -> x5, local copies, waits for them, and re-layouts: 3.06 us -> 4.17 us
where the time goes in v2:
time: 106 us
  Pallas kernels  101 us (95%)
  local copies, waits for them, and re-layouts  4.17 us (4%)
    pallas_call x1, Pallas kernels, shards(): pl.pallas_call(functools.partial(kernel, (owners, rows, cols), tuple(scra...  101 us
    unnamed x5, local copies, waits for them, and re-layouts  4.17 us

profile of v2, /device:TPU:1, one launch (start us, length us, event | category | flops | bytes accessed | tf_op | source)
XLA Modules:
  0.0 106.1 jit_solution(1252212309532187984)
XLA Ops:
  0.6 101.3 %shard_map.76 = (f32[64,16,128]{2,1,0:T(8,128)}, f32[9,9,4,32]{3,2,1,0:T(4,128)}, f32[9,9,4,32]{3,2,1,0:T(4,128)}) custom-call(f32[32,16,128]{2,1,0:T(8,128)} %image.1, f32[64,16,128]{2,1,0:T(8,128)} %warm.1, f32[9,9,32,64]{3,2,1,0:T(8,128)} %bitcast.5, f32[1,64]{1,0:T(1,128)} %bitcast.9, f32[9,9,4,32]{3,2,1,0:T(4,128)} %bitcast.8), custom_call_target="tpu_custom_call" | custom-call | tf_op jit(solution)/shard_map/pallas_call | solution.py:517
  101.9 0.0 copy-start
  101.9 1.9 %copy.11 = f32[64,16,128]{2,1,0:T(8,128)} copy(f32[64,16,128]{2,1,0:T(8,128)} %get-tuple-element.12) | data formatting | bytes 1048576
  103.8 1.6 %copy.12 = f32[4,9,9,32]{3,0,2,1:T(4,128)} copy(f32[4,9,9,32]{3,0,2,1:T(4,128)} %bitcast.7) | data formatting | bytes 82944
  105.4 0.0 copy-done
  105.4 0.7 copy.13
Async XLA Ops:
  101.9 3.5 %copy-start = (f32[9,9,4,32]{3,2,1,0:T(4,128)S(1)}, f32[9,9,4,32]{3,2,1,0:T(4,128)}, u32[]{:S(2)}) copy-start(f32[9,9,4,32]{3,2,1,0:T(4,128)} %get-tuple-element.8) | copy-start | bytes 124420

commit v3 on v2

--- a/solution.py
+++ b/solution.py
@@ -28,6 +28,20 @@
 EXT = ROWS + 8
 SLOTS = EXT + 2
 SCALE = 1.0 / math.sqrt(T * T * C)
+READY = ((0, 8), (8, 16), (16, 26))
+RUNS = (
+    ((0, 4, 0), (4, 8, 4)),
+    ((8, 12, 8), (12, 16, 16)),
+    ((16, 20, 12), (20, 24, 20), (24, 25, -1), (25, 26, -2)),
+)
+PLACE = [0] * EXT
+for _runs in RUNS:
+    for _low, _high, _row in _runs:
+        for _n in range(_high - _low):
+            if _row >= 0:
+                PLACE[_row + _n] = _low + _n
+PARTS = ((0, 10), (10, 18), (18, 26))
+GROUP = 3
 
 
 def split(x):
@@ -47,7 +61,7 @@
     return lane >= shift if shift > 0 else lane < LANES + shift
 
 
-def synthesis(codes, ws, zbuf, acc, part):
+def synthesis(codes, ws, zbuf, acc, part, ready):
     owners = part.shape[0]
     share = C // owners
     lane = lane_index(C)
@@ -93,29 +107,25 @@
             if half == 1 and ho < 8:
                 acc[ho] = main
             else:
-                put(row + 1, main)
-    put(0, rims[0])
-    put(SLOTS - 1, rims[1])
+                put(PLACE[row], main)
+        if ho in (7, 11):
+            ready(ho // 4 - 1)
+    put(24, rims[0])
+    put(25, rims[1])
+    ready(2)
 
 
 def gathered(err, slot):
     return jnp.concatenate([err[q, slot] for q in range(err.shape[0])], axis=0)
 
 
-def adjoint_step(err, wa, level, codes, ebuf, hbuf, qbuf, gbuf):
+def adjoint_step(err, arrived, wa, level, codes, ebuf, hbuf, qbuf, gbuf):
     wide = 3 * C
     lane_c = lane_index(C)
     lane = lane_index(KL)
     spot = lane % 8
-    for row in range(EXT):
-        hi, lo = split(gathered(err, row + 1))
-        for t, side in ((row, 0), (row - 8, 1)):
-            if 0 <= t < 16:
-                cols = slice(side * LANES, (side + 1) * LANES)
-                ebuf[t * wide : t * wide + C, cols] = hi
-                ebuf[t * wide + C : t * wide + 2 * C, cols] = lo
-                ebuf[t * wide + 2 * C : t * wide + 3 * C, cols] = hi
-    rims = [gathered(err, 0), gathered(err, SLOTS - 1)]
+    arrived(0)
+    rims = [gathered(err, 0), gathered(err, 1)]
     for t in range(T):
         hi, lo = split(
             jnp.where(lane_c < LANES - 8 * t, roll(rims[0], -8 * t), roll(rims[1], -8 * t))
@@ -132,6 +142,16 @@
         keep = (spot >= 4) & (spot < 4 + s) if s > 0 else (spot < 4) & (spot >= 4 + s)
         edge = edge + jnp.where(keep, roll(qbuf[b * KL : (b + 1) * KL, 0:LANES], s), 0.0)
     gbuf[...] = edge
+    for row in range(EXT):
+        if row in (8, 16):
+            arrived(row // 8)
+        hi, lo = split(gathered(err, row + 2))
+        for t, side in ((row, 0), (row - 8, 1)):
+            if 0 <= t < 16:
+                cols = slice(side * LANES, (side + 1) * LANES)
+                ebuf[t * wide : t * wide + C, cols] = hi
+                ebuf[t * wide + C : t * wide + 2 * C, cols] = lo
+                ebuf[t * wide + 2 * C : t * wide + 3 * C, cols] = hi
     ends = (lane < 4) | (lane >= LANES - 4)
     bound = level[...]
     for i in range(8):
@@ -150,11 +170,34 @@
             codes[row] = shifted - jnp.clip(shifted, -bound, bound)
 
 
-def correlation(err, codes, lbuf, cbuf, gacc, parts):
+def stacked_codes(codes, cbuf):
+    wide = 3 * LANES
+    none = jnp.zeros((KL, wide), BF16)
+    for i in range(-2, ROWS + 2):
+        inner = 0 <= i < ROWS
+        if inner:
+            hi, lo = split(codes[i])
+        for n in range(GROUP):
+            u = i + 2 - n
+            if not 0 <= u < ROWS + 2:
+                continue
+            rows = slice(n * KL, (n + 1) * KL)
+            if inner:
+                cbuf[rows, u * wide : u * wide + LANES] = hi
+                cbuf[rows, u * wide + LANES : u * wide + 2 * LANES] = lo
+                cbuf[rows, u * wide + 2 * LANES : u * wide + 3 * LANES] = hi
+            else:
+                cbuf[rows, u * wide : (u + 1) * wide] = none
+
+
+def shifted_errors(err, arrived, lbuf):
     lane = lane_index(C)
-    rims = [gathered(err, 0), gathered(err, SLOTS - 1)]
+    arrived(0)
+    rims = [gathered(err, 0), gathered(err, 1)]
     for row in range(EXT):
-        main = gathered(err, row + 1)
+        if row in (8, 16):
+            arrived(row // 8)
+        main = gathered(err, row + 2)
         rim = roll(rims[row // 16], -(8 * (row % 16) + 4))
         for b in range(T):
             s = b - 4
@@ -169,32 +212,25 @@
             lbuf[b * C : (b + 1) * C, at : at + LANES] = hi
             lbuf[b * C : (b + 1) * C, at + LANES : at + 2 * LANES] = hi
             lbuf[b * C : (b + 1) * C, at + 2 * LANES : at + 3 * LANES] = lo
-    none = jnp.zeros((KL, 3 * LANES), BF16)
-    cbuf[0:KL, 0 : 3 * LANES] = none
-    cbuf[ROWS * KL : (ROWS + 1) * KL, 3 * LANES : 6 * LANES] = none
-    for i in range(ROWS):
-        hi, lo = split(codes[i])
-        for at, base in (((i + 1) * KL, 0), (i * KL, 3 * LANES)):
-            cbuf[at : at + KL, base : base + LANES] = hi
-            cbuf[at : at + KL, base + LANES : base + 2 * LANES] = lo
-            cbuf[at : at + KL, base + 2 * LANES : base + 3 * LANES] = hi
-    gacc[...] = jnp.zeros_like(gacc)
-    for row in range(0, EXT, 2):
-        low, high = max(row - 8, -1), min(row, ROWS - 1)
-        a = low - row + 8
-        count = (high - low + 1) * KL
-        gacc[a * KL : a * KL + count] += lax.dot_general(
-            cbuf[(low + 1) * KL : (low + 1) * KL + count],
-            lbuf[:, row * 3 * LANES : (row + 2) * 3 * LANES],
-            (((1,), (1,)), ((), ())),
-            preferred_element_type=F32,
-        )
+
+
+def correlation(group, lbuf, cbuf, gacc, parts):
+    first, depth = group * GROUP, (ROWS + 2) * 3 * LANES
+    start = (6 - first) * 3 * LANES
+    gacc[0 : T * C, 0 : GROUP * KL] = lax.dot_general(
+        lbuf[:, start : start + depth],
+        cbuf[...],
+        (((1,), (1,)), ((), ())),
+        preferred_element_type=F32,
+    )
     groups, share = parts.shape[1], parts.shape[3]
-    for core in range(2):
-        for g in range(groups):
-            for a in range(T):
-                at = a * KL + (2 * g + core) * share
-                parts[core, g, a] = gacc[at : at + share]
+    for m in range(0, 2 * LANES, LANES):
+        for n in range(0, 3 * LANES, LANES):
+            turned = jnp.transpose(gacc[n : n + LANES, m : m + LANES])
+            width = min(LANES, T * C - n)
+            for k in range(0, min(LANES, GROUP * KL - m), share):
+                a, block = first + (m + k) // KL, (k % KL) // share
+                parts[block % 2, block // 2, a, :, n : n + width] = turned[k : k + share, :width]
 
 
 def synthesis_weights(atoms, ws):
@@ -264,23 +300,9 @@
 
 
 def send(src, dst, sems, slot, peer):
-    copy = pltpu.make_async_remote_copy(
-        src_ref=src,
-        dst_ref=dst,
-        send_sem=sems.at[0, slot],
-        recv_sem=sems.at[1, slot],
-        device_id=peer,
-        device_id_type=MESH,
-    )
+    copy = remote(src, dst, sems, slot, peer)
     copy.start()
     return copy
-
-
-def wait_all(copies):
-    for copy in copies:
-        copy.wait_recv()
-    for copy in copies:
-        copy.wait_send()
 
 
 class Grid:
@@ -300,103 +322,147 @@
                     pr, pz = lax.rem(r + dr, rows), lax.rem(self.z + dz, self.halves)
                     place = {"row": pr, "col": 2 * pz + self.core}
                     self.blocks.append((pr * self.halves + pz, place))
+        self.corners = [{**v, **h} for v in (self.up, self.down) for h in (self.left, self.right)]
         self.everyone = self.peers + [self.left, self.right] + [p for _, p in self.blocks]
-
-
-def exchange(grid, part, image, err, rbuf, piece, piece2, h1, msg, h2, field, sems, meanwhile):
-    s_rs, s_h1, s_h2, s_ag = sems
-    owners, rows, cols, share = grid.owners, grid.rows, grid.cols, C // grid.owners
-    copies = [send(part.at[p["atom"]], rbuf.at[d], s_rs, d, p) for d, p in enumerate(grid.peers)]
-    meanwhile()
-    wait_all(copies)
-    total = part[grid.q]
-    for d in range(owners - 1):
-        total = total + rbuf[d]
-    total = total * SCALE
-    piece[0:5] = total[0:5]
-    piece[5:21] = total[5:21] - image[...]
-    piece[21:SLOTS] = total[21:SLOTS]
-
+        self.everyone += self.corners
+
+
+def remote(src, dst, sems, slot, peer):
+    return pltpu.make_async_remote_copy(
+        src_ref=src,
+        dst_ref=dst,
+        send_sem=sems.at[0, slot],
+        recv_sem=sems.at[1, slot],
+        device_id=peer,
+        device_id_type=MESH,
+    )
+
+
+def sum_copies(grid, u, n, chunk):
+    low, high = READY[chunk]
+    count = grid.owners - 1
+    return [
+        remote(
+            u["part"].at[p["atom"], low:high],
+            u["rbuf"].at[n, d, low:high],
+            u["s_rs"].at[n],
+            chunk * count + d,
+            p,
+        )
+        for d, p in enumerate(grid.peers)
+    ]
+
+
+def meet(grid, u, n):
+    share, rows, cols = C // grid.owners, grid.rows, grid.cols
+    piece, field, image = u["piece"], u["field"], u["image"]
+    h1, h2, h3, msg, err = u["h1"].at[n], u["h2"].at[n], u["h3"].at[n], u["msg"], u["err"].at[n]
+    part, rbuf = u["part"], u["rbuf"].at[n]
+    for chunk, runs in enumerate(RUNS):
+        for copy in sum_copies(grid, u, n, chunk):
+            copy.wait_recv()
+        for low, high, row in runs:
+            total = part[grid.q, low:high]
+            for d in range(grid.owners - 1):
+                total = total + rbuf[d, low:high]
+            total = total * SCALE
+            if 4 <= row < 4 + ROWS:
+                total = total - image[row - 4 : row - 4 + high - low]
+            at = row + 1 if row >= 0 else (0 if row == -1 else SLOTS - 1)
+            piece[at : at + high - low] = total
+
+    edges = [
+        send(piece.at[17:26], h1.at[0], u["s_h1"].at[n], 0, grid.down),
+        send(piece.at[0:9], h1.at[1], u["s_h1"].at[n], 1, grid.up),
+    ]
     f_up, f_down = (grid.r > 0).astype(F32), (grid.r < rows - 1).astype(F32)
     f_left, f_right = (grid.c > 0).astype(F32), (grid.c < cols - 1).astype(F32)
     lane = lane_index(share)
-    wait_all(
-        [
-            send(piece.at[17:26], h1.at[0], s_h1, 0, grid.down),
-            send(piece.at[0:9], h1.at[1], s_h1, 1, grid.up),
-        ]
-    )
-    piece2[0] = piece[0] + h1[0, 8] * f_up
-    piece2[1:9] = piece[1:9] + h1[0, 0:8] * f_up
-    piece2[9:17] = piece[9:17]
-    piece2[17:25] = piece[17:25] + h1[1, 1:9] * f_down
-    piece2[25] = piece[25] + jnp.where(lane < 64, h1[1, 0], 0.0) * f_down
-
     ends = (lane < 4) | (lane >= LANES - 4)
     low = lane % 8 < 4
     packed = [jnp.zeros((share, LANES), F32), jnp.zeros((share, LANES), F32)]
     for row in range(EXT):
-        packed[row // 16] += roll(jnp.where(ends, piece2[row + 1], 0.0), 8 * (row % 16) + 4)
-    rims = [piece2[0], piece2[SLOTS - 1]]
+        packed[row // 16] += roll(jnp.where(ends, piece[row + 1], 0.0), 8 * (row % 16) + 4)
+    own = [piece[0], piece[SLOTS - 1]]
     for v in range(2):
-        msg[0, v] = jnp.where(low, packed[v], rims[v])
-        msg[1, v] = jnp.where(low, rims[v], packed[v])
-    wait_all(
-        [
-            send(msg.at[0], h2.at[0], s_h2, 0, grid.right),
-            send(msg.at[1], h2.at[1], s_h2, 1, grid.left),
-        ]
-    )
+        msg[0, v] = jnp.where(low, packed[v], own[v])
+        msg[1, v] = jnp.where(low, own[v], packed[v])
+    edges += [
+        send(msg.at[0, 1], h3.at[0], u["s_h3"].at[n], 0, grid.corners[3]),
+        send(msg.at[0, 0], h3.at[1], u["s_h3"].at[n], 1, grid.corners[1]),
+        send(msg.at[1, 1], h3.at[2], u["s_h3"].at[n], 2, grid.corners[2]),
+        send(msg.at[1, 0], h3.at[3], u["s_h3"].at[n], 3, grid.corners[0]),
+        send(msg.at[0], h2.at[0], u["s_h2"].at[n], 0, grid.right),
+        send(msg.at[1], h2.at[1], u["s_h2"].at[n], 1, grid.left),
+    ]
+    for copy in edges:
+        copy.wait_recv()
+    begin = lane < 64
+    sides = []
+    for side, factor in ((0, f_left), (1, f_right)):
+        above = h3[2 * side] * f_up
+        below = jnp.where(begin, h3[2 * side + 1], 0.0) * f_down
+        sides.append([(h2[side, 0] + above) * factor, (h2[side, 1] + below) * factor])
+    rims = [own[0] + h1[0, 8] * f_up, own[1] + jnp.where(begin, h1[1, 0], 0.0) * f_down]
     inner = [None, None]
     for v in range(2):
-        from_left, from_right = h2[0, v] * f_left, h2[1, v] * f_right
+        from_left, from_right = sides[0][v], sides[1][v]
         rims[v] = rims[v] + jnp.where(low, from_left, from_right)
         inner[v] = jnp.where(low, from_right, from_left)
         rims[v] = rims[v] * jnp.where(low, f_left, f_right)
+    field[0] = rims[0] * jnp.where(lane < 32, f_up, 1.0)
+    field[1] = jnp.where(begin, rims[1] * jnp.where(lane >= 32, f_down, 1.0), 0.0)
+    copies = []
     for row in range(EXT):
         fix = roll(inner[row // 16], -(8 * (row % 16) + 4))
-        value = piece2[row + 1] + jnp.where(ends, fix, 0.0)
+        value = piece[row + 1]
+        if row < 8:
+            value = value + h1[0, row] * f_up
+        if row >= 16:
+            value = value + h1[1, row - 15] * f_down
+        value = value + jnp.where(ends, fix, 0.0)
         if row < 4:
             value = value * f_up
         if row >= EXT - 4:
             value = value * f_down
-        field[row + 1] = value
-    field[0] = rims[0] * jnp.where(lane < 32, f_up, 1.0)
-    field[SLOTS - 1] = jnp.where(lane < 64, rims[1] * jnp.where(lane >= 32, f_down, 1.0), 0.0)
-
-    copies = [send(field, err.at[grid.q], s_ag, d, p) for d, p in enumerate(grid.peers)]
-    err[grid.q] = field[...]
-    wait_all(copies)
-
-
-def update(grid, parts, own, velocity, new_atoms, new_velocity, half, total, chunks, s1, s2):
-    wait_all([send(parts.at[1 - grid.core], half, s1, 0, grid.partner)])
-    total[...] = parts[grid.core] + half[...]
-    wait_all([send(total.at[g], chunks.at[d], s2, d, p) for d, (g, p) in enumerate(grid.blocks)])
-    summed = total[grid.r * grid.halves + grid.z]
-    for d in range(len(grid.blocks)):
-        summed = summed + chunks[d]
-    pixels = ROWS * LANES * grid.rows * grid.cols
-    summed = summed * (1.0 / pixels)
-    square = None
-    for b in range(T):
-        cols = slice(b * C, (b + 1) * C)
-        fresh = MOMENTUM * velocity[:, b] + summed[:, :, cols]
-        stepped = own[:, :, cols] - LEARN_RATE * fresh
-        new_velocity[:, b] = fresh
-        new_atoms[:, b] = stepped
-        term = jnp.sum(stepped * stepped, axis=0)
-        square = term if square is None else square + term
-    square = jnp.sum(square, axis=1, keepdims=True) * (1.0 / (T * T * C))
-    gain = lax.rsqrt(square + EPSILON)
-    for b in range(T):
-        new_atoms[:, b] = new_atoms[:, b] * gain[None]
-
-
-def kernel(sizes, names, image, warm, atoms, limits, velocity, new_codes, new_atoms, new_velocity, *scratch):
+        field[row + 2] = value
+        if row % 8 == 7:
+            chunk = row // 8
+            first, last = PARTS[chunk]
+            copies.append(
+                [
+                    send(
+                        field.at[first:last],
+                        err.at[grid.q, first:last],
+                        u["s_ag"].at[n],
+                        chunk * (grid.owners - 1) + d,
+                        p,
+                    )
+                    for d, p in enumerate(grid.peers)
+                ]
+            )
+            err[grid.q, first:last] = field[first:last]
+    for chunk in range(len(READY)):
+        for copy in sum_copies(grid, u, n, chunk):
+            copy.wait_send()
+    for copy in edges:
+        copy.wait_send()
+
+    def arrived(chunk):
+        for copy in copies[chunk]:
+            copy.wait_recv()
+        if chunk == 2:
+            for group in copies:
+                for copy in group:
+                    copy.wait_send()
+
+    return arrived
+
+
+def kernel(sizes, names, owned, image, warm, atoms, limits, new_codes, grad, picked, *scratch):
     u = dict(zip(names, scratch))
     grid = Grid(*sizes)
-    share, owned = C // grid.owners, velocity.shape[2]
+    share = C // grid.owners
     greet(grid.everyone)
     codes = u["codes"]
     loads = [pltpu.make_async_copy(atoms, u["atoms"], u["s_in"].at[0])]
@@ -416,51 +482,95 @@
     synthesis_weights(u["atoms"], u["ws"])
     for load in loads[1:]:
         load.wait()
-    synthesis(codes, u["ws"], u["zbuf"], u["acc"], u["part"])
-
-    def meet(n, meanwhile):
-        exchange(
-            grid,
-            u["part"],
-            u["image"],
-            u["err"].at[n],
-            u["rbuf"].at[n],
-            u["piece"],
-            u["piece2"],
-            u["h1"].at[n],
-            u["msg"],
-            u["h2"].at[n],
-            u["field"],
-            [u[s].at[n] for s in ("s_rs", "s_h1", "s_h2", "s_ag")],
-            meanwhile,
-        )
-
-    def prepare():
-        adjoint_weights(u["atoms"], u["flip"], u["wa"])
-        start = (grid.r * grid.cols + grid.c) * owned
-        owned_atoms(u["atoms"], start, owned, u["own"])
-
-    greeted(grid.everyone)
-    meet(0, prepare)
+
+    def partial_sums(n, begin):
+        def ready(chunk):
+            if chunk == 0:
+                begin()
+            for copy in sum_copies(grid, u, n, chunk):
+                copy.start()
+
+        synthesis(codes, u["ws"], u["zbuf"], u["acc"], u["part"], ready)
+
+    partial_sums(0, lambda: greeted(grid.everyone))
+    adjoint_weights(u["atoms"], u["flip"], u["wa"])
+    owned_atoms(u["atoms"], (grid.r * grid.cols + grid.c) * owned, owned, picked)
 
     def one(n, carry):
+        arrived = meet(grid, u, n)
         buffers = [u[s] for s in ("ebuf", "hbuf", "qbuf", "gbuf")]
-        adjoint_step(u["err"].at[n - 1], u["wa"], u["level"], codes, *buffers)
-        synthesis(codes, u["ws"], u["zbuf"], u["acc"], u["part"])
-        meet(n, lambda: None)
+        adjoint_step(u["err"].at[n], arrived, u["wa"], u["level"], codes, *buffers)
+        partial_sums(n + 1, lambda: None)
         return carry
 
-    lax.fori_loop(1, ITERS + 1, one, 0)
+    lax.fori_loop(0, ITERS, one, 0)
     stores = [
         pltpu.make_async_copy(codes.at[i], new_codes.at[:, i], u["s_in"].at[i]) for i in range(ROWS)
     ]
     for store in stores:
         store.start()
-    correlation(u["err"].at[ITERS], codes, u["lbuf"], u["cbuf"], u["gacc"], u["parts"])
-    buffers = [u[s] for s in ("half", "total", "chunks", "s_core", "s_block")]
-    update(grid, u["parts"], u["own"], velocity, new_atoms, new_velocity, *buffers)
+    stacked_codes(codes, u["cbuf"])
+    arrived = meet(grid, u, ITERS)
+    shifted_errors(u["err"].at[ITERS], arrived, u["lbuf"])
+
+    parts, half, total, chunks = (u[s] for s in ("parts", "half", "total", "chunks"))
+    pairs, blocks = [], []
+
+    def taps(group):
+        return slice(group * GROUP, (group + 1) * GROUP)
+
+    def spread(group):
+        pairs[group].wait_recv()
+        at = taps(group)
+        total[:, at] = parts[grid.core, :, at] + half[:, at]
+        for d, (g, p) in enumerate(grid.blocks):
+            slot = group * len(grid.blocks) + d
+            blocks.append(send(total.at[g, at], chunks.at[d, at], u["s_block"], slot, p))
+
+    for group in range(T // GROUP):
+        correlation(group, u["lbuf"], u["cbuf"], u["gacc"], parts)
+        at = taps(group)
+        pairs.append(
+            send(parts.at[1 - grid.core, :, at], half.at[:, at], u["s_core"], group, grid.partner)
+        )
+        if group > 0:
+            spread(group - 1)
+    spread(T // GROUP - 1)
+    pixels = ROWS * LANES * grid.rows * grid.cols
+    for group in range(T // GROUP):
+        at = taps(group)
+        for copy in blocks[group * len(grid.blocks) : (group + 1) * len(grid.blocks)]:
+            copy.wait_recv()
+        summed = total[grid.r * grid.halves + grid.z, at]
+        for d in range(len(grid.blocks)):
+            summed = summed + chunks[d, at]
+        grad[at] = summed * (1.0 / pixels)
+    for copy in pairs + blocks:
+        copy.wait_send()
     for store in stores:
         store.wait()
+
+
+def finish(codes, grad, own, velocity, new_codes, new_atoms, new_velocity, buffer, sems):
+    read = pltpu.make_async_copy(codes, buffer, sems.at[0])
+    read.start()
+    square = None
+    for b in range(T):
+        cols = slice(b * C, (b + 1) * C)
+        fresh = MOMENTUM * velocity[:, b] + grad[:, :, cols]
+        stepped = own[:, :, cols] - LEARN_RATE * fresh
+        new_velocity[:, b] = fresh
+        new_atoms[:, b] = stepped
+        term = jnp.sum(stepped * stepped, axis=0)
+        square = term if square is None else square + term
+    read.wait()
+    write = pltpu.make_async_copy(buffer, new_codes, sems.at[1])
+    write.start()
+    square = jnp.sum(square, axis=1, keepdims=True) * (1.0 / (T * T * C))
+    gain = lax.rsqrt(square + EPSILON)
+    for b in range(T):
+        new_atoms[:, b] = new_atoms[:, b] * gain[None]
+    write.wait()
 
 
 def struct(shape, dtype=F32):
@@ -482,54 +592,55 @@
         "ws": pltpu.VMEM((T * C, (T + 1) * 3 * KL), BF16),
         "flip": pltpu.VMEM((7 * LANES, 5 * LANES), F32),
         "wa": pltpu.VMEM((T * KL, 7 * LANES), BF16),
-        "own": pltpu.VMEM(chunk, F32),
         "zbuf": pltpu.VMEM((10 * 3 * KL, 2 * LANES), BF16),
         "acc": pltpu.VMEM((8, C, LANES), F32),
         "part": pltpu.VMEM((owners, SLOTS, share, LANES), F32),
         "err": pltpu.VMEM((rounds, owners, SLOTS, share, LANES), F32),
         "rbuf": pltpu.VMEM((rounds, owners - 1, SLOTS, share, LANES), F32),
         "piece": piece,
-        "piece2": piece,
         "h1": pltpu.VMEM((rounds, 2, 9, share, LANES), F32),
         "msg": pltpu.VMEM((2, 2, share, LANES), F32),
         "h2": pltpu.VMEM((rounds, 2, 2, share, LANES), F32),
+        "h3": pltpu.VMEM((rounds, 4, share, LANES), F32),
         "field": piece,
         "ebuf": pltpu.VMEM((16 * 3 * C, 2 * LANES), BF16),
         "hbuf": pltpu.VMEM((T * 3 * C, LANES), BF16),
         "qbuf": pltpu.VMEM((T * KL, 2 * LANES), F32),
         "gbuf": pltpu.VMEM((KL, LANES), F32),
         "lbuf": pltpu.VMEM((T * C, EXT * 3 * LANES), BF16),
-        "cbuf": pltpu.VMEM(((ROWS + 1) * KL, 6 * LANES), BF16),
-        "gacc": pltpu.VMEM((T * KL, T * C), F32),
+        "cbuf": pltpu.VMEM((GROUP * KL, (ROWS + 2) * 3 * LANES), BF16),
+        "gacc": pltpu.VMEM((3 * LANES, 2 * LANES), F32),
         "parts": pltpu.VMEM((2, groups) + chunk, F32),
         "half": pltpu.VMEM((groups,) + chunk, F32),
         "total": pltpu.VMEM((groups,) + chunk, F32),
         "chunks": pltpu.VMEM((groups - 1,) + chunk, F32),
         "s_in": sems((1 + 2 * ROWS,)),
-        "s_rs": sems((rounds, 2, owners - 1)),
+        "s_rs": sems((rounds, 2, 3 * (owners - 1))),
         "s_h1": sems((rounds, 2, 2)),
         "s_h2": sems((rounds, 2, 2)),
-        "s_ag": sems((rounds, 2, owners - 1)),
-        "s_core": sems((2, 1)),
-        "s_block": sems((2, groups - 1)),
+        "s_h3": sems((rounds, 2, 4)),
+        "s_ag": sems((rounds, 2, 3 * (owners - 1))),
+        "s_core": sems((2, T // GROUP)),
+        "s_block": sems((2, T // GROUP * (groups - 1))),
     }
     natural = (T, T, owned, C)
-    new_codes, new_atoms, new_velocity = pl.pallas_call(
-        functools.partial(kernel, (owners, rows, cols), tuple(scratch)),
-        out_shape=(struct((KL, ROWS, LANES)), struct(natural), struct(natural)),
-        in_specs=[ANY, ANY, ANY, VMEM, VMEM],
+    codes, grad, own = pl.pallas_call(
+        functools.partial(kernel, (owners, rows, cols), tuple(scratch), owned),
+        out_shape=(struct((KL, ROWS, LANES)), struct(chunk), struct(chunk)),
+        in_specs=[ANY, ANY, ANY, VMEM],
         out_specs=(ANY, VMEM, VMEM),
         scratch_shapes=list(scratch.values()),
         compiler_params=pltpu.CompilerParams(
             vmem_limit_bytes=60 << 20, collective_id=0, has_side_effects=True
         ),
-    )(
-        hyper_image,
-        warm_codes,
-        dictionary.transpose(1, 2, 3, 0),
-        thresholds.reshape(1, KL),
-        velocity.transpose(1, 2, 0, 3),
-    )
+    )(hyper_image, warm_codes, dictionary.transpose(1, 2, 3, 0), thresholds.reshape(1, KL))
+    new_codes, new_atoms, new_velocity = pl.pallas_call(
+        finish,
+        out_shape=(struct((KL, ROWS, LANES)), struct(natural), struct(natural)),
+        in_specs=[ANY, VMEM, VMEM, VMEM],
+        out_specs=(ANY, VMEM, VMEM),
+        scratch_shapes=[pltpu.VMEM((KL, ROWS, LANES), F32), sems((2,))],
+    )(codes, grad, own, velocity.transpose(1, 2, 0, 3))
     return new_codes, new_atoms.transpose(2, 0, 1, 3), new_velocity.transpose(2, 0, 1, 3)
 
 

time: 106 us -> 97.7 us (0.922)
  Pallas kernels: 101 us -> 96.7 us
  local copies, waits for them, and re-layouts: 4.17 us -> 0 us
    pallas_call x1, Pallas kernels: 101 us -> 93.1 us  [shards(): pl.pallas_call(functools.partial(kernel, (owners, rows, cols), tuple(scra...]
    unnamed x5 -> x0, local copies, waits for them, and re-layouts: 4.17 us -> none
    pallas_call x0 -> x1, Pallas kernels: none -> 3.56 us  [shards(): pl.pallas_call(finish, out_shape=(struct((KL, ROWS, LANES)), struct(natur...]
where the time goes in v3:
time: 97.7 us; the launch traced here: 97.5 us
  Pallas kernels  96.7 us (99%)
    pallas_call x1, Pallas kernels, shards(): pl.pallas_call(functools.partial(kernel, (owners, rows, cols), tuple(scra...  93.1 us
    pallas_call x1, Pallas kernels, shards(): pl.pallas_call(finish, out_shape=(struct((KL, ROWS, LANES)), struct(natur...  3.56 us

profile of v3, /device:TPU:1, one launch (start us, length us, event | category | flops | bytes accessed | tf_op | source)
XLA Modules:
  0.0 97.5 jit_solution(15636472277214400527)
XLA Ops:
  0.6 93.1 %shard_map.76 = (f32[64,16,128]{2,1,0:T(8,128)}, f32[9,4,288]{2,1,0:T(4,128)}, f32[9,4,288]{2,1,0:T(4,128)}) custom-call(f32[32,16,128]{2,1,0:T(8,128)} %image.1, f32[64,16,128]{2,1,0:T(8,128)} %warm.1, f32[9,9,32,64]{3,2,1,0:T(8,128)} %bitcast.5, f32[1,64]{1,0:T(1,128)} %bitcast.7), custom_call_target="tpu_custom_call" | custom-call | tf_op jit(solution)/shard_map/pallas_call | solution.py:627
  93.7 3.6 %shard_map.77 = (f32[64,16,128]{2,1,0:T(8,128)}, f32[9,9,4,32]{3,2,1,0:T(4,128)}, f32[9,9,4,32]{3,2,1,0:T(4,128)}) custom-call(f32[64,16,128]{2,1,0:T(8,128)} %get-tuple-element.9.codes, f32[9,4,288]{2,1,0:T(4,128)} %get-tuple-element.10.grad, f32[9,4,288]{2,1,0:T(4,128)} %get-tuple-element.11.own, f32[9,9,4,32]{3,2,1,0:T(4,128)} %bitcast.6), custom_call_target="tpu_custom_call" | custom-call | tf_op jit(solution)/shard_map/pallas_call | solution.py:637

commit v4 on v3

--- a/solution.py
+++ b/solution.py
@@ -28,11 +28,13 @@
 EXT = ROWS + 8
 SLOTS = EXT + 2
 SCALE = 1.0 / math.sqrt(T * T * C)
-READY = ((0, 8), (8, 16), (16, 26))
+READY = ((0, 8), (8, 16), (16, 20), (20, 26))
+STEPS = (7, 11, 13, 15)
 RUNS = (
     ((0, 4, 0), (4, 8, 4)),
     ((8, 12, 8), (12, 16, 16)),
-    ((16, 20, 12), (20, 24, 20), (24, 25, -1), (25, 26, -2)),
+    ((16, 18, 12), (18, 20, 20)),
+    ((20, 22, 14), (22, 24, 22), (24, 25, -1), (25, 26, -2)),
 )
 PLACE = [0] * EXT
 for _runs in RUNS:
@@ -40,7 +42,15 @@
         for _n in range(_high - _low):
             if _row >= 0:
                 PLACE[_row + _n] = _low + _n
-PARTS = ((0, 10), (10, 18), (18, 26))
+PARTS = ((0, 12), (12, 19), (19, 27))
+LAST = (16, 23)
+FIELD = 19
+
+
+def spot(row):
+    return row + 3 if row < 8 else row + 11 if row < 16 else row - 5
+
+
 GROUP = 3
 
 
@@ -108,22 +118,31 @@
                 acc[ho] = main
             else:
                 put(PLACE[row], main)
-        if ho in (7, 11):
-            ready(ho // 4 - 1)
+        if ho in STEPS[:-1]:
+            ready(STEPS.index(ho))
     put(24, rims[0])
     put(25, rims[1])
-    ready(2)
+    ready(len(STEPS) - 1)
 
 
 def gathered(err, slot):
     return jnp.concatenate([err[q, slot] for q in range(err.shape[0])], axis=0)
 
 
-def adjoint_step(err, arrived, wa, level, codes, ebuf, hbuf, qbuf, gbuf):
+def error_row(err, row, fix):
+    main = gathered(err, spot(row))
+    if 8 <= row < 16:
+        lane = lane_index(C)
+        ends = (lane < 4) | (lane >= LANES - 4)
+        main = main + jnp.where(ends, roll(fix, -(8 * row + 4)), 0.0)
+    return main
+
+
+def adjoint_step(err, arrived, wa, level, codes, ebuf, hbuf, qbuf, qbuf2, gbuf):
     wide = 3 * C
     lane_c = lane_index(C)
     lane = lane_index(KL)
-    spot = lane % 8
+    place = lane % 8
     arrived(0)
     rims = [gathered(err, 0), gathered(err, 1)]
     for t in range(T):
@@ -139,35 +158,59 @@
         s = b - 4
         if s == 0:
             continue
-        keep = (spot >= 4) & (spot < 4 + s) if s > 0 else (spot < 4) & (spot >= 4 + s)
+        keep = (place >= 4) & (place < 4 + s) if s > 0 else (place < 4) & (place >= 4 + s)
         edge = edge + jnp.where(keep, roll(qbuf[b * KL : (b + 1) * KL, 0:LANES], s), 0.0)
     gbuf[...] = edge
-    for row in range(EXT):
-        if row in (8, 16):
-            arrived(row // 8)
-        hi, lo = split(gathered(err, row + 2))
-        for t, side in ((row, 0), (row - 8, 1)):
-            if 0 <= t < 16:
-                cols = slice(side * LANES, (side + 1) * LANES)
-                ebuf[t * wide : t * wide + C, cols] = hi
-                ebuf[t * wide + C : t * wide + 2 * C, cols] = lo
-                ebuf[t * wide + 2 * C : t * wide + 3 * C, cols] = hi
+
+    def take(first, last):
+        fix = gathered(err, 2)
+        for row in range(first, last + 1):
+            hi, lo = split(error_row(err, row, fix))
+            for t, side in ((row, 0), (row - 8, 1)):
+                if 0 <= t < 16:
+                    cols = slice(side * LANES, (side + 1) * LANES)
+                    ebuf[t * wide : t * wide + C, cols] = hi
+                    ebuf[t * wide + C : t * wide + 2 * C, cols] = lo
+                    ebuf[t * wide + 2 * C : t * wide + 3 * C, cols] = hi
+
+    arrived(2)
+    take(0, LAST[0])
     ends = (lane < 4) | (lane >= LANES - 4)
-    bound = level[...]
-    for i in range(8):
-        qbuf[...] = jnp.dot(
-            wa[:, 0 : T * wide], ebuf[i * wide : (i + T) * wide], preferred_element_type=F32
+
+    def multiply(i, out):
+        start = pl.multiple_of(i * wide, wide)
+        out[...] = jnp.dot(
+            wa[:, 0 : T * wide], ebuf[pl.ds(start, T * wide)], preferred_element_type=F32
         )
+
+    def shrink(i, taps):
+        bound = level[...]
         for half in range(2):
             row = i + 8 * half
-            total = jnp.where(ends, roll(gbuf[...], -(8 * row + 4)), 0.0)
+            back = LANES - 4 - 64 * half - 8 * i
+            total = jnp.where(ends, pltpu.roll(gbuf[...], back, 1), 0.0)
             for b in range(T):
-                moved = roll(qbuf[b * KL : (b + 1) * KL, half * LANES : (half + 1) * LANES], b - 4)
+                moved = roll(taps[b * KL : (b + 1) * KL, half * LANES : (half + 1) * LANES], b - 4)
                 if b != 4:
                     moved = jnp.where(inside(lane, b - 4), moved, 0.0)
                 total = total + moved
             shifted = codes[row] - (ETA_CODE * SCALE) * total
             codes[row] = shifted - jnp.clip(shifted, -bound, bound)
+
+    def two(n, carry):
+        multiply(2 * n + 1, qbuf2)
+        shrink(2 * n, qbuf)
+        multiply(2 * n + 2, qbuf)
+        shrink(2 * n + 1, qbuf2)
+        return carry
+
+    multiply(0, qbuf)
+    arrived(1)
+    take(LAST[0] + 1, LAST[1])
+    lax.fori_loop(0, 3, two, 0)
+    multiply(7, qbuf2)
+    shrink(6, qbuf)
+    shrink(7, qbuf2)
 
 
 def stacked_codes(codes, cbuf):
@@ -190,14 +233,17 @@
                 cbuf[rows, u * wide : (u + 1) * wide] = none
 
 
-def shifted_errors(err, arrived, lbuf):
+def shifted_errors(err, arrived, lbuf, first, last):
     lane = lane_index(C)
-    arrived(0)
+    if first == 0:
+        arrived(0)
+        arrived(2)
+    fix = gathered(err, 2)
     rims = [gathered(err, 0), gathered(err, 1)]
-    for row in range(EXT):
-        if row in (8, 16):
-            arrived(row // 8)
-        main = gathered(err, row + 2)
+    for row in range(first, last):
+        if row - 1 == LAST[0]:
+            arrived(1)
+        main = error_row(err, row, fix)
         rim = roll(rims[row // 16], -(8 * (row % 16) + 4))
         for b in range(T):
             s = b - 4
@@ -233,11 +279,12 @@
                 parts[block % 2, block // 2, a, :, n : n + width] = turned[k : k + share, :width]
 
 
-def synthesis_weights(atoms, ws):
+def synthesis_weights(atoms, ws, taken):
     for a in range(0, T + 1, 2):
         pairs = []
         for t in (a, a + 1):
             if t < T:
+                taken(t)
                 field = jnp.concatenate([atoms[t, b] for b in range(T)], axis=0)
                 hi, lo = split(field)
                 pairs += [hi.astype(F32), hi.astype(F32), lo.astype(F32)]
@@ -299,10 +346,19 @@
     pl.semaphore_wait(pltpu.get_barrier_semaphore(), len(peers))
 
 
-def send(src, dst, sems, slot, peer):
-    copy = remote(src, dst, sems, slot, peer)
-    copy.start()
-    return copy
+def remote(src, dst, sems, peer):
+    return pltpu.make_async_remote_copy(
+        src_ref=src,
+        dst_ref=dst,
+        send_sem=sems.at[0],
+        recv_sem=sems.at[1],
+        device_id=peer,
+        device_id_type=MESH,
+    )
+
+
+def send(src, dst, sems, peer):
+    remote(src, dst, sems, peer).start()
 
 
 class Grid:
@@ -327,83 +383,71 @@
         self.everyone += self.corners
 
 
-def remote(src, dst, sems, slot, peer):
-    return pltpu.make_async_remote_copy(
-        src_ref=src,
-        dst_ref=dst,
-        send_sem=sems.at[0, slot],
-        recv_sem=sems.at[1, slot],
-        device_id=peer,
-        device_id_type=MESH,
-    )
-
-
-def sum_copies(grid, u, n, chunk):
+def send_sums(grid, u, n, chunk):
     low, high = READY[chunk]
-    count = grid.owners - 1
-    return [
-        remote(
-            u["part"].at[p["atom"], low:high],
-            u["rbuf"].at[n, d, low:high],
-            u["s_rs"].at[n],
-            chunk * count + d,
-            p,
-        )
-        for d, p in enumerate(grid.peers)
-    ]
+    for d, p in enumerate(grid.peers):
+        source = u["part"].at[p["atom"], low:high]
+        send(source, u["rbuf"].at[n, d, low:high], u["s_rs"].at[n, chunk], p)
+
+
+def all_of(ref, sems, peer):
+    return remote(ref, ref, sems, peer)
 
 
 def meet(grid, u, n):
     share, rows, cols = C // grid.owners, grid.rows, grid.cols
     piece, field, image = u["piece"], u["field"], u["image"]
-    h1, h2, h3, msg, err = u["h1"].at[n], u["h2"].at[n], u["h3"].at[n], u["msg"], u["err"].at[n]
+    rim, msg, err = u["rim"].at[n], u["msg"], u["err"].at[n]
+    h1, h2, h3 = rim.at[0:18], rim.at[18:22], rim.at[22:26]
+    someone = grid.partner
     part, rbuf = u["part"], u["rbuf"].at[n]
-    for chunk, runs in enumerate(RUNS):
-        for copy in sum_copies(grid, u, n, chunk):
-            copy.wait_recv()
-        for low, high, row in runs:
-            total = part[grid.q, low:high]
-            for d in range(grid.owners - 1):
-                total = total + rbuf[d, low:high]
-            total = total * SCALE
-            if 4 <= row < 4 + ROWS:
-                total = total - image[row - 4 : row - 4 + high - low]
-            at = row + 1 if row >= 0 else (0 if row == -1 else SLOTS - 1)
-            piece[at : at + high - low] = total
-
-    edges = [
-        send(piece.at[17:26], h1.at[0], u["s_h1"].at[n], 0, grid.down),
-        send(piece.at[0:9], h1.at[1], u["s_h1"].at[n], 1, grid.up),
-    ]
-    f_up, f_down = (grid.r > 0).astype(F32), (grid.r < rows - 1).astype(F32)
-    f_left, f_right = (grid.c > 0).astype(F32), (grid.c < cols - 1).astype(F32)
     lane = lane_index(share)
     ends = (lane < 4) | (lane >= LANES - 4)
     low = lane % 8 < 4
     packed = [jnp.zeros((share, LANES), F32), jnp.zeros((share, LANES), F32)]
-    for row in range(EXT):
-        packed[row // 16] += roll(jnp.where(ends, piece[row + 1], 0.0), 8 * (row % 16) + 4)
+    for chunk, runs in enumerate(RUNS):
+        first, last = READY[chunk]
+        all_of(rbuf.at[:, first:last], u["s_rs"].at[n, chunk], someone).wait_recv()
+        for begin, end, row in runs:
+            total = part[grid.q, begin:end]
+            for d in range(grid.owners - 1):
+                total = total + rbuf[d, begin:end]
+            total = total * SCALE
+            if 4 <= row < 4 + ROWS:
+                total = total - image[row - 4 : row - 4 + end - begin]
+            at = row + 1 if row >= 0 else (0 if row == -1 else SLOTS - 1)
+            piece[at : at + end - begin] = total
+            for k in range(end - begin if row >= 0 else 0):
+                edge = jnp.where(ends, total[k], 0.0)
+                packed[(row + k) // 16] += roll(edge, 8 * ((row + k) % 16) + 4)
+
+    s_rim = u["s_rim"].at[n]
+    send(piece.at[17:26], h1.at[0:9], s_rim, grid.down)
+    send(piece.at[0:9], h1.at[9:18], s_rim, grid.up)
+    f_up, f_down = (grid.r > 0).astype(F32), (grid.r < rows - 1).astype(F32)
+    f_left, f_right = (grid.c > 0).astype(F32), (grid.c < cols - 1).astype(F32)
     own = [piece[0], piece[SLOTS - 1]]
     for v in range(2):
-        msg[0, v] = jnp.where(low, packed[v], own[v])
-        msg[1, v] = jnp.where(low, own[v], packed[v])
-    edges += [
-        send(msg.at[0, 1], h3.at[0], u["s_h3"].at[n], 0, grid.corners[3]),
-        send(msg.at[0, 0], h3.at[1], u["s_h3"].at[n], 1, grid.corners[1]),
-        send(msg.at[1, 1], h3.at[2], u["s_h3"].at[n], 2, grid.corners[2]),
-        send(msg.at[1, 0], h3.at[3], u["s_h3"].at[n], 3, grid.corners[0]),
-        send(msg.at[0], h2.at[0], u["s_h2"].at[n], 0, grid.right),
-        send(msg.at[1], h2.at[1], u["s_h2"].at[n], 1, grid.left),
-    ]
-    for copy in edges:
-        copy.wait_recv()
+        msg[v] = jnp.where(low, packed[v], own[v])
+        msg[2 + v] = jnp.where(low, own[v], packed[v])
+    send(msg.at[1], h3.at[0], s_rim, grid.corners[3])
+    send(msg.at[0], h3.at[1], s_rim, grid.corners[1])
+    send(msg.at[3], h3.at[2], s_rim, grid.corners[2])
+    send(msg.at[2], h3.at[3], s_rim, grid.corners[0])
+    send(msg.at[0:2], h2.at[0:2], s_rim, grid.right)
+    send(msg.at[2:4], h2.at[2:4], s_rim, grid.left)
+    first, last = PARTS[2]
+    for p in grid.peers:
+        send(piece.at[9:17], err.at[grid.q, first:last], u["s_ag"].at[n, 2], p)
+    err[grid.q, first:last] = piece[9:17]
+    all_of(rim, s_rim, someone).wait_recv()
     begin = lane < 64
     sides = []
     for side, factor in ((0, f_left), (1, f_right)):
         above = h3[2 * side] * f_up
         below = jnp.where(begin, h3[2 * side + 1], 0.0) * f_down
-        sides.append([(h2[side, 0] + above) * factor, (h2[side, 1] + below) * factor])
-    rims = [own[0] + h1[0, 8] * f_up, own[1] + jnp.where(begin, h1[1, 0], 0.0) * f_down]
+        sides.append([(h2[2 * side] + above) * factor, (h2[2 * side + 1] + below) * factor])
+    rims = [own[0] + h1[8] * f_up, own[1] + jnp.where(begin, h1[9], 0.0) * f_down]
     inner = [None, None]
     for v in range(2):
         from_left, from_right = sides[0][v], sides[1][v]
@@ -412,49 +456,36 @@
         rims[v] = rims[v] * jnp.where(low, f_left, f_right)
     field[0] = rims[0] * jnp.where(lane < 32, f_up, 1.0)
     field[1] = jnp.where(begin, rims[1] * jnp.where(lane >= 32, f_down, 1.0), 0.0)
-    copies = []
-    for row in range(EXT):
+    field[2] = inner[0]
+    for row in (*range(8), *range(16, EXT)):
         fix = roll(inner[row // 16], -(8 * (row % 16) + 4))
         value = piece[row + 1]
         if row < 8:
-            value = value + h1[0, row] * f_up
+            value = value + h1[row] * f_up
         if row >= 16:
-            value = value + h1[1, row - 15] * f_down
+            value = value + h1[row - 6] * f_down
         value = value + jnp.where(ends, fix, 0.0)
         if row < 4:
             value = value * f_up
         if row >= EXT - 4:
             value = value * f_down
-        field[row + 2] = value
-        if row % 8 == 7:
-            chunk = row // 8
+        field[spot(row)] = value
+        if row in LAST:
+            chunk = LAST.index(row)
             first, last = PARTS[chunk]
-            copies.append(
-                [
-                    send(
-                        field.at[first:last],
-                        err.at[grid.q, first:last],
-                        u["s_ag"].at[n],
-                        chunk * (grid.owners - 1) + d,
-                        p,
-                    )
-                    for d, p in enumerate(grid.peers)
-                ]
-            )
+            for p in grid.peers:
+                send(field.at[first:last], err.at[grid.q, first:last], u["s_ag"].at[n, chunk], p)
             err[grid.q, first:last] = field[first:last]
-    for chunk in range(len(READY)):
-        for copy in sum_copies(grid, u, n, chunk):
-            copy.wait_send()
-    for copy in edges:
-        copy.wait_send()
+    for chunk, (first, last) in enumerate(READY):
+        all_of(rbuf.at[:, first:last], u["s_rs"].at[n, chunk], someone).wait_send()
+    all_of(rim, s_rim, someone).wait_send()
 
     def arrived(chunk):
-        for copy in copies[chunk]:
-            copy.wait_recv()
-        if chunk == 2:
-            for group in copies:
-                for copy in group:
-                    copy.wait_send()
+        first, last = PARTS[chunk]
+        all_of(rbuf.at[:, 0 : last - first], u["s_ag"].at[n, chunk], someone).wait_recv()
+        if chunk == 1:
+            for other, (first, last) in enumerate(PARTS):
+                all_of(rbuf.at[:, 0 : last - first], u["s_ag"].at[n, other], someone).wait_send()
 
     return arrived
 
@@ -465,30 +496,30 @@
     share = C // grid.owners
     greet(grid.everyone)
     codes = u["codes"]
-    loads = [pltpu.make_async_copy(atoms, u["atoms"], u["s_in"].at[0])]
+    loads = [
+        pltpu.make_async_copy(atoms.at[a], u["atoms"].at[a], u["s_atoms"].at[a]) for a in range(T)
+    ]
+    for load in loads:
+        load.start()
     for i in range(ROWS):
-        loads.append(pltpu.make_async_copy(warm.at[:, i], codes.at[i], u["s_in"].at[1 + i]))
+        pltpu.make_async_copy(warm.at[:, i], codes.at[i], u["s_in"].at[1]).start()
     for i in range(ROWS):
         bands = image.at[pl.ds(grid.q * share, share), i]
-        loads.append(pltpu.make_async_copy(bands, u["image"].at[i], u["s_in"].at[1 + ROWS + i]))
-    for load in loads:
-        load.start()
+        pltpu.make_async_copy(bands, u["image"].at[i], u["s_in"].at[2]).start()
     diagonal = lax.broadcasted_iota(jnp.int32, (KL, KL), 0) == lax.broadcasted_iota(
         jnp.int32, (KL, KL), 1
     )
     column = jnp.sum(jnp.where(diagonal, limits[...], 0.0), axis=1, keepdims=True)
     u["level"][...] = jnp.broadcast_to(ETA_CODE * column, (KL, LANES))
-    loads[0].wait()
-    synthesis_weights(u["atoms"], u["ws"])
-    for load in loads[1:]:
-        load.wait()
+    synthesis_weights(u["atoms"], u["ws"], lambda a: loads[a].wait())
+    pltpu.make_async_copy(codes, codes, u["s_in"].at[1]).wait()
+    pltpu.make_async_copy(u["image"], u["image"], u["s_in"].at[2]).wait()
 
     def partial_sums(n, begin):
         def ready(chunk):
             if chunk == 0:
                 begin()
-            for copy in sum_copies(grid, u, n, chunk):
-                copy.start()
+            send_sums(grid, u, n, chunk)
 
         synthesis(codes, u["ws"], u["zbuf"], u["acc"], u["part"], ready)
 
@@ -498,62 +529,72 @@
 
     def one(n, carry):
         arrived = meet(grid, u, n)
-        buffers = [u[s] for s in ("ebuf", "hbuf", "qbuf", "gbuf")]
+        buffers = [u[s] for s in ("ebuf", "hbuf", "qbuf", "qbuf2", "gbuf")]
         adjoint_step(u["err"].at[n], arrived, u["wa"], u["level"], codes, *buffers)
         partial_sums(n + 1, lambda: None)
         return carry
 
     lax.fori_loop(0, ITERS, one, 0)
-    stores = [
-        pltpu.make_async_copy(codes.at[i], new_codes.at[:, i], u["s_in"].at[i]) for i in range(ROWS)
-    ]
-    for store in stores:
-        store.start()
+    for i in range(ROWS):
+        pltpu.make_async_copy(codes.at[i], new_codes.at[:, i], u["s_in"].at[3]).start()
     stacked_codes(codes, u["cbuf"])
     arrived = meet(grid, u, ITERS)
-    shifted_errors(u["err"].at[ITERS], arrived, u["lbuf"])
-
+    err, lbuf = u["err"].at[ITERS], u["lbuf"]
     parts, half, total, chunks = (u[s] for s in ("parts", "half", "total", "chunks"))
-    pairs, blocks = [], []
 
     def taps(group):
         return slice(group * GROUP, (group + 1) * GROUP)
 
     def spread(group):
-        pairs[group].wait_recv()
-        at = taps(group)
+        at, s_core = taps(group), u["s_core"].at[group]
+        all_of(half.at[:, at], s_core, grid.partner).wait_recv()
         total[:, at] = parts[grid.core, :, at] + half[:, at]
         for d, (g, p) in enumerate(grid.blocks):
-            slot = group * len(grid.blocks) + d
-            blocks.append(send(total.at[g, at], chunks.at[d, at], u["s_block"], slot, p))
-
-    for group in range(T // GROUP):
-        correlation(group, u["lbuf"], u["cbuf"], u["gacc"], parts)
+            send(total.at[g, at], chunks.at[d, at], u["s_block"].at[group], p)
+
+    def correlate(group):
+        correlation(group, lbuf, u["cbuf"], u["gacc"], parts)
         at = taps(group)
-        pairs.append(
-            send(parts.at[1 - grid.core, :, at], half.at[:, at], u["s_core"], group, grid.partner)
-        )
-        if group > 0:
-            spread(group - 1)
-    spread(T // GROUP - 1)
+        send(parts.at[1 - grid.core, :, at], half.at[:, at], u["s_core"].at[group], grid.partner)
+
+    shifted_errors(err, arrived, lbuf, 0, 18)
+    correlate(2)
+    shifted_errors(err, arrived, lbuf, 18, EXT)
+    correlate(1)
+    spread(2)
+    correlate(0)
+    spread(1)
+    spread(0)
     pixels = ROWS * LANES * grid.rows * grid.cols
-    for group in range(T // GROUP):
+    for group in (2, 1, 0):
         at = taps(group)
-        for copy in blocks[group * len(grid.blocks) : (group + 1) * len(grid.blocks)]:
-            copy.wait_recv()
+        all_of(chunks.at[:, at], u["s_block"].at[group], grid.partner).wait_recv()
         summed = total[grid.r * grid.halves + grid.z, at]
         for d in range(len(grid.blocks)):
             summed = summed + chunks[d, at]
         grad[at] = summed * (1.0 / pixels)
-    for copy in pairs + blocks:
-        copy.wait_send()
-    for store in stores:
-        store.wait()
+    for group in range(T // GROUP):
+        at = taps(group)
+        all_of(half.at[:, at], u["s_core"].at[group], grid.partner).wait_send()
+        all_of(chunks.at[:, at], u["s_block"].at[group], grid.partner).wait_send()
+    pltpu.make_async_copy(codes, codes, u["s_in"].at[3]).wait()
 
 
 def finish(codes, grad, own, velocity, new_codes, new_atoms, new_velocity, buffer, sems):
-    read = pltpu.make_async_copy(codes, buffer, sems.at[0])
-    read.start()
+    pieces = [pl.ds(n * (KL // 4), KL // 4) for n in range(4)]
+    reads = [
+        pltpu.make_async_copy(codes.at[at], buffer.at[at], sems.at[0, n])
+        for n, at in enumerate(pieces)
+    ]
+    writes = [
+        pltpu.make_async_copy(buffer.at[at], new_codes.at[at], sems.at[1, n])
+        for n, at in enumerate(pieces)
+    ]
+    for read in reads:
+        read.start()
+    for read, write in zip(reads, writes):
+        read.wait()
+        write.start()
     square = None
     for b in range(T):
         cols = slice(b * C, (b + 1) * C)
@@ -563,14 +604,12 @@
         new_atoms[:, b] = stepped
         term = jnp.sum(stepped * stepped, axis=0)
         square = term if square is None else square + term
-    read.wait()
-    write = pltpu.make_async_copy(buffer, new_codes, sems.at[1])
-    write.start()
     square = jnp.sum(square, axis=1, keepdims=True) * (1.0 / (T * T * C))
     gain = lax.rsqrt(square + EPSILON)
     for b in range(T):
         new_atoms[:, b] = new_atoms[:, b] * gain[None]
-    write.wait()
+    for write in writes:
+        write.wait()
 
 
 def struct(shape, dtype=F32):
@@ -595,17 +634,16 @@
         "zbuf": pltpu.VMEM((10 * 3 * KL, 2 * LANES), BF16),
         "acc": pltpu.VMEM((8, C, LANES), F32),
         "part": pltpu.VMEM((owners, SLOTS, share, LANES), F32),
-        "err": pltpu.VMEM((rounds, owners, SLOTS, share, LANES), F32),
+        "err": pltpu.VMEM((rounds, owners, FIELD + 8, share, LANES), F32),
         "rbuf": pltpu.VMEM((rounds, owners - 1, SLOTS, share, LANES), F32),
         "piece": piece,
-        "h1": pltpu.VMEM((rounds, 2, 9, share, LANES), F32),
-        "msg": pltpu.VMEM((2, 2, share, LANES), F32),
-        "h2": pltpu.VMEM((rounds, 2, 2, share, LANES), F32),
-        "h3": pltpu.VMEM((rounds, 4, share, LANES), F32),
-        "field": piece,
+        "rim": pltpu.VMEM((rounds, 26, share, LANES), F32),
+        "msg": pltpu.VMEM((4, share, LANES), F32),
+        "field": pltpu.VMEM((FIELD, share, LANES), F32),
         "ebuf": pltpu.VMEM((16 * 3 * C, 2 * LANES), BF16),
         "hbuf": pltpu.VMEM((T * 3 * C, LANES), BF16),
         "qbuf": pltpu.VMEM((T * KL, 2 * LANES), F32),
+        "qbuf2": pltpu.VMEM((T * KL, 2 * LANES), F32),
         "gbuf": pltpu.VMEM((KL, LANES), F32),
         "lbuf": pltpu.VMEM((T * C, EXT * 3 * LANES), BF16),
         "cbuf": pltpu.VMEM((GROUP * KL, (ROWS + 2) * 3 * LANES), BF16),
@@ -614,14 +652,13 @@
         "half": pltpu.VMEM((groups,) + chunk, F32),
         "total": pltpu.VMEM((groups,) + chunk, F32),
         "chunks": pltpu.VMEM((groups - 1,) + chunk, F32),
-        "s_in": sems((1 + 2 * ROWS,)),
-        "s_rs": sems((rounds, 2, 3 * (owners - 1))),
-        "s_h1": sems((rounds, 2, 2)),
-        "s_h2": sems((rounds, 2, 2)),
-        "s_h3": sems((rounds, 2, 4)),
-        "s_ag": sems((rounds, 2, 3 * (owners - 1))),
-        "s_core": sems((2, T // GROUP)),
-        "s_block": sems((2, T // GROUP * (groups - 1))),
+        "s_in": sems((4,)),
+        "s_atoms": sems((T,)),
+        "s_rs": sems((rounds, len(READY), 2)),
+        "s_rim": sems((rounds, 2)),
+        "s_ag": sems((rounds, len(PARTS), 2)),
+        "s_core": sems((T // GROUP, 2)),
+        "s_block": sems((T // GROUP, 2)),
     }
     natural = (T, T, owned, C)
     codes, grad, own = pl.pallas_call(
@@ -639,7 +676,7 @@
         out_shape=(struct((KL, ROWS, LANES)), struct(natural), struct(natural)),
         in_specs=[ANY, VMEM, VMEM, VMEM],
         out_specs=(ANY, VMEM, VMEM),
-        scratch_shapes=[pltpu.VMEM((KL, ROWS, LANES), F32), sems((2,))],
+        scratch_shapes=[pltpu.VMEM((KL, ROWS, LANES), F32), sems((2, 4))],
     )(codes, grad, own, velocity.transpose(1, 2, 0, 3))
     return new_codes, new_atoms.transpose(2, 0, 1, 3), new_velocity.transpose(2, 0, 1, 3)
 

time: 97.7 us -> 95 us (0.972)
  Pallas kernels: 96.7 us -> 94 us
    pallas_call x1, Pallas kernels: 93.1 us -> 90.5 us  [shards(): pl.pallas_call(functools.partial(kernel, (owners, rows, cols), tuple(scra...]
where the time goes in v4:
time: 95 us; the launch traced here: 94.8 us
  Pallas kernels  94 us (99%)
    pallas_call x1, Pallas kernels, shards(): pl.pallas_call(functools.partial(kernel, (owners, rows, cols), tuple(scra...  90.5 us
    pallas_call x1, Pallas kernels, shards(): pl.pallas_call(finish, out_shape=(struct((KL, ROWS, LANES)), struct(natur...  3.53 us

profile of v4, /device:TPU:1, one launch (start us, length us, event | category | flops | bytes accessed | tf_op | source)
XLA Modules:
  0.0 94.8 jit_solution(5726460200905488207)
XLA Ops:
  0.6 90.5 %shard_map.76 = (f32[64,16,128]{2,1,0:T(8,128)}, f32[9,4,288]{2,1,0:T(4,128)}, f32[9,4,288]{2,1,0:T(4,128)}) custom-call(f32[32,16,128]{2,1,0:T(8,128)} %image.1, f32[64,16,128]{2,1,0:T(8,128)} %warm.1, f32[9,9,32,64]{3,2,1,0:T(8,128)} %bitcast.5, f32[1,64]{1,0:T(1,128)} %bitcast.7), custom_call_target="tpu_custom_call" | custom-call | tf_op jit(solution)/shard_map/pallas_call | solution.py:664
  91.1 3.5 %shard_map.77 = (f32[64,16,128]{2,1,0:T(8,128)}, f32[9,9,4,32]{3,2,1,0:T(4,128)}, f32[9,9,4,32]{3,2,1,0:T(4,128)}) custom-call(f32[64,16,128]{2,1,0:T(8,128)} %get-tuple-element.9.codes, f32[9,4,288]{2,1,0:T(4,128)} %get-tuple-element.10.grad, f32[9,4,288]{2,1,0:T(4,128)} %get-tuple-element.11.own, f32[9,9,4,32]{3,2,1,0:T(4,128)} %bitcast.6), custom_call_target="tpu_custom_call" | custom-call | tf_op jit(solution)/shard_map/pallas_call | solution.py:674

commit v5 on v4

--- a/solution.py
+++ b/solution.py
@@ -422,8 +422,6 @@
                 packed[(row + k) // 16] += roll(edge, 8 * ((row + k) % 16) + 4)
 
     s_rim = u["s_rim"].at[n]
-    send(piece.at[17:26], h1.at[0:9], s_rim, grid.down)
-    send(piece.at[0:9], h1.at[9:18], s_rim, grid.up)
     f_up, f_down = (grid.r > 0).astype(F32), (grid.r < rows - 1).astype(F32)
     f_left, f_right = (grid.c > 0).astype(F32), (grid.c < cols - 1).astype(F32)
     own = [piece[0], piece[SLOTS - 1]]
@@ -436,6 +434,8 @@
     send(msg.at[2], h3.at[3], s_rim, grid.corners[0])
     send(msg.at[0:2], h2.at[0:2], s_rim, grid.right)
     send(msg.at[2:4], h2.at[2:4], s_rim, grid.left)
+    send(piece.at[17:26], h1.at[0:9], s_rim, grid.down)
+    send(piece.at[0:9], h1.at[9:18], s_rim, grid.up)
     first, last = PARTS[2]
     for p in grid.peers:
         send(piece.at[9:17], err.at[grid.q, first:last], u["s_ag"].at[n, 2], p)

time: 95 us -> 94.4 us (level)
  no operation moved by 1% of the time
where the time goes in v5:
time: 94.4 us; the launch traced here: 94.2 us
  Pallas kernels  93.4 us (99%)
    pallas_call x1, Pallas kernels, shards(): pl.pallas_call(functools.partial(kernel, (owners, rows, cols), tuple(scra...  89.9 us
    pallas_call x1, Pallas kernels, shards(): pl.pallas_call(finish, out_shape=(struct((KL, ROWS, LANES)), struct(natur...  3.53 us

profile of v5, /device:TPU:1, one launch (start us, length us, event | category | flops | bytes accessed | tf_op | source)
XLA Modules:
  0.0 94.2 jit_solution(15406036310992669420)
XLA Ops:
  0.6 89.9 %shard_map.76 = (f32[64,16,128]{2,1,0:T(8,128)}, f32[9,4,288]{2,1,0:T(4,128)}, f32[9,4,288]{2,1,0:T(4,128)}) custom-call(f32[32,16,128]{2,1,0:T(8,128)} %image.1, f32[64,16,128]{2,1,0:T(8,128)} %warm.1, f32[9,9,32,64]{3,2,1,0:T(8,128)} %bitcast.5, f32[1,64]{1,0:T(1,128)} %bitcast.7), custom_call_target="tpu_custom_call" | custom-call | tf_op jit(solution)/shard_map/pallas_call | solution.py:664
  90.5 3.5 %shard_map.77 = (f32[64,16,128]{2,1,0:T(8,128)}, f32[9,9,4,32]{3,2,1,0:T(4,128)}, f32[9,9,4,32]{3,2,1,0:T(4,128)}) custom-call(f32[64,16,128]{2,1,0:T(8,128)} %get-tuple-element.9.codes, f32[9,4,288]{2,1,0:T(4,128)} %get-tuple-element.10.grad, f32[9,4,288]{2,1,0:T(4,128)} %get-tuple-element.11.own, f32[9,9,4,32]{3,2,1,0:T(4,128)} %bitcast.6), custom_call_target="tpu_custom_call" | custom-call | tf_op jit(solution)/shard_map/pallas_call | solution.py:674
